TPU v7x, 256 devices: a whole 4x4x8 slice. The times are simulated.
256 devices in a mesh: px: 8 (over x, core), py: 32 (over z, y).
Axes of the slice: x: 4, y: 4, z: 8, core: 2. Of those that a mesh axis runs over, the one named last changes fastest.
Arguments:
- field: float32 [5, 64, 512, 128], P(None, 'px', 'py'), may hold values from -6 to 6
- forcing: float32 [5, 64, 512, 128], P(None, 'px', 'py'), may hold values from -6 to 6
- x_inverse: float32 [5, 5, 64, 512, 128], P(None, None, 'px', 'py'), may hold values from -1 to 1
- x_lower: float32 [5, 5, 64, 512, 128], P(None, None, 'px', 'py'), may hold values from -1 to 1
- x_upper: float32 [5, 5, 64, 512, 128], P(None, None, 'px', 'py'), may hold values from -1 to 1
- y_inverse: float32 [5, 5, 64, 512, 128], P(None, None, 'px', 'py'), may hold values from -1 to 1
- y_lower: float32 [5, 5, 64, 512, 128], P(None, None, 'px', 'py'), may hold values from -1 to 1
- y_upper: float32 [5, 5, 64, 512, 128], P(None, None, 'px', 'py'), may hold values from -1 to 1
Outputs:
- update: float32 [5, 64, 512, 128], P(None, 'px', 'py')
All inputs are finite; a program needn't handle non-finite values.
Results may differ from a plain program's by a relative error of at most 0.00014.
Values sent between devices are 32-bit elements; how exact they have to be, the bound alone decides.
A program may use at most 64 MiB of HBM per device.

v0:
```python
import jax
import jax.numpy as jnp
from jax import lax
from jax.sharding import PartitionSpec as P

DISSIPATION = 0.1


def from_behind(value, axis, steps):
    count = lax.axis_size(axis)
    first, last = (max(0, -steps), min(count, count - steps))
    return lax.ppermute(value, axis, [(source, source + steps) for source in range(first, last)])


def extended(shard, sides, width):
    for axis, dim in sides:
        devices, length = (lax.axis_size(axis), shard.shape[dim])
        up = [(i, (i + 1) % devices) for i in range(devices - 1)]
        down = [(j, i) for i, j in up]
        last = lax.slice_in_dim(shard, length - width, length, axis=dim)
        first = lax.slice_in_dim(shard, 0, width, axis=dim)
        before = lax.ppermute(last, axis, up)
        after = lax.ppermute(first, axis, down)
        shard = jnp.concatenate([before, shard, after], axis=dim)
    return shard


def apply_block(blocks, vector):
    return jnp.sum(blocks * vector[None], axis=1)


def block_product(later, earlier):
    return jnp.sum(later[:, :, None] * earlier[None, :, :], axis=1)


def compose_cells(source, coupling, line_axis, backward):
    length = source.shape[line_axis]
    start = jnp.zeros(source.shape[:line_axis] + source.shape[line_axis + 1 :], jnp.float32)
    unit_matrix = jnp.eye(source.shape[0], dtype=jnp.float32)[:, :, None, None]
    start_matrix = jnp.broadcast_to(
        unit_matrix, (source.shape[0], source.shape[0]) + start.shape[1:]
    )

    def compose_advance(i, carried):
        matrix, vector = carried
        k = length - 1 - i if backward else i
        here = lax.dynamic_index_in_dim(coupling, k, line_axis + 1, keepdims=False)
        inflow = lax.dynamic_index_in_dim(source, k, line_axis, keepdims=False)
        return (-block_product(here, matrix), inflow - apply_block(here, vector))

    return lax.fori_loop(0, length, compose_advance, (start_matrix, start))


def run_cells(source, coupling, inflow, line_axis, backward):
    length = source.shape[line_axis]

    def run_advance(i, carried):
        before, result = carried
        k = length - 1 - i if backward else i
        here = lax.dynamic_index_in_dim(coupling, k, line_axis + 1, keepdims=False)
        current = lax.dynamic_index_in_dim(source, k, line_axis, keepdims=False) - apply_block(
            here, before
        )
        return (current, lax.dynamic_update_index_in_dim(result, current, k, line_axis))

    return lax.fori_loop(0, length, run_advance, (inflow, jnp.zeros_like(source)))[1]


def carry_x_forward(matrix, vector):

    def relay_step(i, inflow):
        return from_behind(apply_block(matrix, inflow) + vector, "px", 1)

    return lax.fori_loop(0, lax.axis_size("px") - 1, relay_step, jnp.zeros_like(vector))


def carry_x_backward(matrix, vector):

    def relay_step(i, inflow):
        return from_behind(apply_block(matrix, inflow) + vector, "px", -1)

    return lax.fori_loop(0, lax.axis_size("px") - 1, relay_step, jnp.zeros_like(vector))


def carry_y_forward(matrix, vector):

    def relay_step(i, inflow):
        return from_behind(apply_block(matrix, inflow) + vector, "py", 1)

    return lax.fori_loop(0, lax.axis_size("py") - 1, relay_step, jnp.zeros_like(vector))


def carry_y_backward(matrix, vector):

    def relay_step(i, inflow):
        return from_behind(apply_block(matrix, inflow) + vector, "py", -1)

    return lax.fori_loop(0, lax.axis_size("py") - 1, relay_step, jnp.zeros_like(vector))


def per_device(field, forcing, x_inverse, x_lower, x_upper, y_inverse, y_lower, y_upper):
    cells_x = field.shape[1]
    cells_y = field.shape[2]
    padded = extended(field, (("px", 1), ("py", 2)), 2)

    def window_x(k):
        return padded[:, k : k + cells_x, 2 : 2 + cells_y]

    def window_y(k):
        return padded[:, 2 : 2 + cells_x, k : k + cells_y]

    along_x = window_x(0) - 4.0 * window_x(1) + 6.0 * window_x(2) - 4.0 * window_x(3) + window_x(4)
    along_y = window_y(0) - 4.0 * window_y(1) + 6.0 * window_y(2) - 4.0 * window_y(3) + window_y(4)
    rhs = forcing - DISSIPATION * (along_x + along_y)
    source = apply_block(x_inverse, rhs)
    matrix, vector = compose_cells(source, x_lower, 1, False)
    inflow = carry_x_forward(matrix, vector)
    forward = run_cells(source, x_lower, inflow, 1, False)
    matrix, vector = compose_cells(forward, x_upper, 1, True)
    inflow = carry_x_backward(matrix, vector)
    x_result = run_cells(forward, x_upper, inflow, 1, True)
    source = apply_block(y_inverse, x_result)
    matrix, vector = compose_cells(source, y_lower, 2, False)
    inflow = carry_y_forward(matrix, vector)
    forward = run_cells(source, y_lower, inflow, 2, False)
    matrix, vector = compose_cells(forward, y_upper, 2, True)
    inflow = carry_y_backward(matrix, vector)
    return run_cells(forward, y_upper, inflow, 2, True)


def solution(mesh):
    in_specs = (
        P(None, "px", "py", None),
        P(None, "px", "py", None),
        P(None, None, "px", "py", None),
        P(None, None, "px", "py", None),
        P(None, None, "px", "py", None),
        P(None, None, "px", "py", None),
        P(None, None, "px", "py", None),
        P(None, None, "px", "py", None),
    )
    out_specs = P(None, "px", "py", None)
    return jax.shard_map(
        per_device, mesh=mesh, in_specs=in_specs, out_specs=out_specs, check_vma=False
    )
```

profile of v0, /device:TPU:124, one launch (start us, length us, event | category | flops | bytes accessed | tf_op | source)
XLA Modules:
  0.0 780.2 jit_solution(5930805934858634255)
XLA Ops:
  16.3 7.9 %collective-permute-done.7 = f32[5,12,2,128]{3,2,1,0:T(2,128)S(1)} collective-permute-done((f32[5,12,2,128]{3,2,1,0:T(2,128)}, f32[5,12,2,128]{3,2,1,0:T(2,128)S(1)}, u32[]{:S(2)}, u32[]{:S(2)}) %collective-permute-start.7) | collective-permute-done | bytes 61472 | tf_op jit(solution)/shard_map/ppermute | solution.py:23
  25.8 9.0 %while.180 = (s32[]{:T(128)}, f32[5,5,16,128]{3,2,1,0:T(8,128)S(1)}, f32[5,16,128]{2,1,0:T(8,128)S(1)}, f32[5,5,8,16,128]{4,3,2,1,0:T(8,128)}, f32[5,8,16,128]{3,2,1,0:T(8,128)S(1)}, /*index=5*/s32[]{:T(128)}, s32[]{:T(128)}) while((s32[]{:T(128)}, f32[5,5,16,128]{3,2,1,0:T(8,128)S(1)}, f32[5,16,128]{2,1,0:T(8,128)S(1)}, ...), condition=%wide.region_4.5_spmd.clone, body=%wide.region_1.4_spmd.clone.sunk | while | flops 624643 | bytes 1720415 | solution.py:51
  34.8 37.5 %while.172 = (s32[]{:T(128)}, f32[5,16,128]{2,1,0:T(8,128)S(1)}, f32[5,5,16,128]{3,2,1,0:T(8,128)S(1)}, f32[5,16,128]{2,1,0:T(8,128)S(1)}, s32[]{:T(128)}) while((s32[]{:T(128)}, f32[5,16,128]{2,1,0:T(8,128)S(1)}, f32[5,5,16,128]{3,2,1,0:T(8,128)S(1)}, f32[5,16,128]{2,1,0:T(8,128)S(1)}, s32[]{:T(128)}) %tuple.314), condition=%wide.region_7.8_spmd, body=%wide.region_5.7_spmd.sunk | while | flops 102402 | bytes 573541 | solution.py:74
  72.4 8.2 %while.173 = (s32[]{:T(128)}, f32[5,16,128]{2,1,0:T(8,128)S(1)}, f32[5,8,16,128]{3,2,1,0:T(8,128)S(1)}, f32[5,8,16,128]{3,2,1,0:T(8,128)S(1)}, f32[5,5,8,16,128]{4,3,2,1,0:T(8,128)}, /*index=5*/s32[]{:T(128)}) while((s32[]{:T(128)}, f32[5,16,128]{2,1,0:T(8,128)S(1)}, f32[5,8,16,128]{3,2,1,0:T(8,128)S(1)}, f32[5,8,16,128]{3,2,1,0:T(8,128)S(1)}, ...), condition=%wide.region_10.11_spmd, body=%wide.region_8.10_spmd.sunk | while | flops 112642 | bytes 532561 | solution.py:66
  80.7 9.2 %while.181 = (s32[]{:T(128)}, f32[5,5,16,128]{3,2,1,0:T(8,128)S(1)}, f32[5,16,128]{2,1,0:T(8,128)S(1)}, f32[5,5,8,16,128]{4,3,2,1,0:T(8,128)}, f32[5,8,16,128]{3...) while((s32[]{:T(128)}, f32[5,5,16,128]{3,2,1,0:T(8,128)S(1)}, ...), condition=%wide.region_14.15_spmd.clone, body=%wide.region_11.14_spmd.clone.sunk | while | flops 624647 | bytes 1720477 | solution.py:51
  89.9 35.8 %while.174 = (s32[]{:T(128)}, f32[5,16,128]{2,1,0:T(8,128)S(1)}, f32[5,5,16,128]{3,2,1,0:T(8,128)S(1)}, f32[5,16,128]{2,1,0:T(8,128)S(1)}, s32[]{:T(128)}) while((s32[]{:T(128)}, f32[5,16,128]{2,1,0:T(8,128)S(1)}, f32[5,5,16,128]{3,2,1,0:T(8,128)S(1)}, f32[5,16,128]{2,1,0:T(8,128)S(1)}, s32[]{:T(128)}) %tuple.323), condition=%wide.region_17.18_spmd, body=%wide.region_15.17_spmd.sunk | while | flops 102402 | bytes 573541 | solution.py:82
  125.7 8.2 %while.175 = (s32[]{:T(128)}, f32[5,16,128]{2,1,0:T(8,128)S(1)}, f32[5,8,16,128]{3,2,1,0:T(8,128)S(1)}, f32[5,8,16,128]{3,2,1,0:T(8,128)S(1)}, f32[5,5,8,16,128]...) while((s32[]{:T(128)}, f32[5,16,128]{2,1,0:T(8,128)S(1)}, ...), condition=%wide.region_20.21_spmd, body=%wide.region_18.20_spmd.sunk | while | flops 112646 | bytes 532631 | solution.py:66
  134.2 22.2 %while.182 = (s32[]{:T(128)}, f32[5,5,8,128]{3,2,1,0:T(8,128)S(1)}, f32[5,8,128]{2,1,0:T(8,128)S(1)}, f32[5,5,8,16,128]{4,3,2,1,0:T(8,128)}, f32[5,8,16,128]{3,2,1,0:T(8,128)S(1)}, /*index=5*/s32[]{:T(128)}, s32[]{:T(128)}) while((s32[]{:T(128)}, f32[5,5,8,128]{3,2,1,0:T(8,128)S(1)}, f32[5,8,128]{2,1,0:T(8,128)S(1)}, ...), condition=%wide.region_25.26_spmd.clone, body=%wide.region_22.25_spmd.clone.sunk | while | flops 312323 | bytes 1003615 | solution.py:51
  156.4 274.5 %while.176 = (s32[]{:T(128)}, f32[5,8,128]{2,1,0:T(8,128)S(1)}, f32[5,5,8,128]{3,2,1,0:T(8,128)S(1)}, f32[5,8,128]{2,1,0:T(8,128)S(1)}, s32[]{:T(128)}) while((s32[]{:T(128)}, f32[5,8,128]{2,1,0:T(8,128)S(1)}, f32[5,5,8,128]{3,2,1,0:T(8,128)S(1)}, f32[5,8,128]{2,1,0:T(8,128)S(1)}, s32[]{:T(128)}) %tuple.332), condition=%wide.region_28.29_spmd, body=%wide.region_26.28_spmd.sunk | while | flops 51202 | bytes 286821 | solution.py:90
  169.0 7.5 collective-permute-start.2
  178.0 7.5 collective-permute-start.2
  187.1 7.5 collective-permute-start.2
  196.1 7.5 collective-permute-start.2
  205.1 7.5 collective-permute-start.2
  214.1 7.5 collective-permute-start.2
  223.2 7.6 collective-permute-start.2
  232.3 7.5 collective-permute-start.2
  241.3 7.5 collective-permute-start.2
  250.3 7.5 collective-permute-start.2
  259.4 7.5 collective-permute-start.2
  268.4 7.5 collective-permute-start.2
  277.4 7.5 collective-permute-start.2
  286.4 7.6 collective-permute-start.2
  295.5 7.5 collective-permute-start.2
  304.6 7.5 collective-permute-start.2
  313.6 7.5 collective-permute-start.2
  322.6 7.5 collective-permute-start.2
  331.6 7.5 collective-permute-start.2
  340.7 7.5 collective-permute-start.2
  349.7 7.6 collective-permute-start.2
  358.8 7.5 collective-permute-start.2
  367.8 7.5 collective-permute-start.2
  376.8 7.5 collective-permute-start.2
  385.9 7.5 collective-permute-start.2
  394.9 7.5 collective-permute-start.2
  403.9 7.5 collective-permute-start.2
  412.9 7.5 collective-permute-start.2
  422.0 7.5 collective-permute-start.2
  431.0 22.8 %while.177 = (s32[]{:T(128)}, f32[5,8,128]{2,1,0:T(8,128)S(1)}, f32[5,8,16,128]{3,2,1,0:T(8,128)S(1)}, f32[5,8,16,128]{3,2,1,0:T(8,128)S(1)}, f32[5,5,8,16,128]{4,3,2,1,0:T(8,128)}, /*index=5*/s32[]{:T(128)}, s32[]{:T(128)}) while((s32[]{:T(128)}, f32[5,8,128]{2,1,0:T(8,128)S(1)}, f32[5,8,16,128]{3,2,1,0:T(8,128)S(1)}, ...), condition=%wide.region_31.32_spmd, body=%wide.region_29.31_spmd.sunk | while | flops 56322 | bytes 532569 | solution.py:66
  453.9 22.3 %while.183 = (s32[]{:T(128)}, f32[5,5,8,128]{3,2,1,0:T(8,128)S(1)}, f32[5,8,128]{2,1,0:T(8,128)S(1)}, f32[5,5,8,16,128]{4,3,2,1,0:T(8,128)}, f32[5,8,16,128]{3,2...) while((s32[]{:T(128)}, f32[5,5,8,128]{3,2,1,0:T(8,128)S(1)}, ...), condition=%wide.region_35.36_spmd.clone, body=%wide.region_32.35_spmd.clone.sunk | while | flops 312327 | bytes 1003677 | solution.py:51
  476.2 280.2 %while.178 = (s32[]{:T(128)}, f32[5,8,128]{2,1,0:T(8,128)S(1)}, f32[5,5,8,128]{3,2,1,0:T(8,128)S(1)}, f32[5,8,128]{2,1,0:T(8,128)S(1)}, s32[]{:T(128)}) while((s32[]{:T(128)}, f32[5,8,128]{2,1,0:T(8,128)S(1)}, f32[5,5,8,128]{3,2,1,0:T(8,128)S(1)}, f32[5,8,128]{2,1,0:T(8,128)S(1)}, s32[]{:T(128)}) %tuple.341), condition=%wide.region_38.39_spmd, body=%wide.region_36.38_spmd.sunk | while | flops 51202 | bytes 286821 | solution.py:98
  478.2 7.4 collective-permute-done.3
  487.5 7.1 collective-permute-done.3
  496.5 7.1 collective-permute-done.3
  523.6 7.1 collective-permute-done.3
  577.8 7.2 collective-permute-done.3
  641.0 7.2 collective-permute-done.3
  756.5 23.0 %while.179 = (s32[]{:T(128)}, f32[5,8,128]{2,1,0:T(8,128)S(1)}, f32[5,8,16,128]{3,2,1,0:T(8,128)S(1)}, f32[5,8,16,128]{3,2,1,0:T(8,128)S(1)}, f32[5,5,8,16,128]{...) while((s32[]{:T(128)}, f32[5,8,128]{2,1,0:T(8,128)S(1)}, ...), condition=%wide.region_41.42_spmd, body=%wide.region_39.41_spmd.sunk | while | flops 56326 | bytes 532631 | solution.py:66
  (821 shorter events, 503.6 us)
Async XLA Ops:
  14.0 10.2 %collective-permute-start.7 = (f32[5,12,2,128]{3,2,1,0:T(2,128)}, f32[5,12,2,128]{3,2,1,0:T(2,128)S(1)}, u32[]{:S(2)}, u32[]{:S(2)}) collective-permute-start(f32[5,12,2,128]{3,2,1,0:T(2,128)} %get-tuple-element.1230), channel_id=1, source_target_pairs={{1,0},{2,1},{3,2},{4,3},{5,4},{6,5},{7,6},{8,7},{9,8},{10,9},{11,1... | collective-permute-start | bytes 184328 | tf_op jit(solution)/shard_map/ppermute | solution.py:23
  169.0 9.0 %collective-permute-start.2 = (f32[5,8,128]{2,1,0:T(8,128)S(1)}, f32[5,8,128]{2,1,0:T(8,128)S(1)}, u32[]{:S(2)}, u32[]{:S(2)}) collective-permute-start(f32[5,8,128]{2,1,0:T(8,128)S(1)} %add.327), channel_id=1, source_target_pairs={{0,1},{1,2},{2,3},{3,4},{4,5},{5,6},{6,7},{7,8},{8,9},{9,10},{10,1... | collective-permute-start | bytes 61448 | tf_op jit(solution)/shard_map/while/body/eval_jaxpr/ppermute | solution.py:12
  178.0 9.0 %collective-permute-start.2 = (f32[5,8,128]{2,1,0:T(8,128)S(1)}, f32[5,8,128]{2,1,0:T(8,128)S(1)}, u32[]{:S(2)}, u32[]{:S(2)}) collective-permute-start(f32[5,8,128]{2,1,0:T(8,128)S(1)} %add.327), channel_id=1, source_target_pairs={{0,1},{1,2},{2,3},{3,4},{4,5},{5,6},{6,7},{7,8},{8,9},{9,10},{10,1... | collective-permute-start | bytes 61448 | tf_op jit(solution)/shard_map/while/body/eval_jaxpr/ppermute | solution.py:12
  187.1 9.0 %collective-permute-start.2 = (f32[5,8,128]{2,1,0:T(8,128)S(1)}, f32[5,8,128]{2,1,0:T(8,128)S(1)}, u32[]{:S(2)}, u32[]{:S(2)}) collective-permute-start(f32[5,8,128]{2,1,0:T(8,128)S(1)} %add.327), channel_id=1, source_target_pairs={{0,1},{1,2},{2,3},{3,4},{4,5},{5,6},{6,7},{7,8},{8,9},{9,10},{10,1... | collective-permute-start | bytes 61448 | tf_op jit(solution)/shard_map/while/body/eval_jaxpr/ppermute | solution.py:12
  196.1 9.0 %collective-permute-start.2 = (f32[5,8,128]{2,1,0:T(8,128)S(1)}, f32[5,8,128]{2,1,0:T(8,128)S(1)}, u32[]{:S(2)}, u32[]{:S(2)}) collective-permute-start(f32[5,8,128]{2,1,0:T(8,128)S(1)} %add.327), channel_id=1, source_target_pairs={{0,1},{1,2},{2,3},{3,4},{4,5},{5,6},{6,7},{7,8},{8,9},{9,10},{10,1... | collective-permute-start | bytes 61448 | tf_op jit(solution)/shard_map/while/body/eval_jaxpr/ppermute | solution.py:12
  205.1 9.0 %collective-permute-start.2 = (f32[5,8,128]{2,1,0:T(8,128)S(1)}, f32[5,8,128]{2,1,0:T(8,128)S(1)}, u32[]{:S(2)}, u32[]{:S(2)}) collective-permute-start(f32[5,8,128]{2,1,0:T(8,128)S(1)} %add.327), channel_id=1, source_target_pairs={{0,1},{1,2},{2,3},{3,4},{4,5},{5,6},{6,7},{7,8},{8,9},{9,10},{10,1... | collective-permute-start | bytes 61448 | tf_op jit(solution)/shard_map/while/body/eval_jaxpr/ppermute | solution.py:12
  214.1 9.0 %collective-permute-start.2 = (f32[5,8,128]{2,1,0:T(8,128)S(1)}, f32[5,8,128]{2,1,0:T(8,128)S(1)}, u32[]{:S(2)}, u32[]{:S(2)}) collective-permute-start(f32[5,8,128]{2,1,0:T(8,128)S(1)} %add.327), channel_id=1, source_target_pairs={{0,1},{1,2},{2,3},{3,4},{4,5},{5,6},{6,7},{7,8},{8,9},{9,10},{10,1... | collective-permute-start | bytes 61448 | tf_op jit(solution)/shard_map/while/body/eval_jaxpr/ppermute | solution.py:12
  223.2 9.1 %collective-permute-start.2 = (f32[5,8,128]{2,1,0:T(8,128)S(1)}, f32[5,8,128]{2,1,0:T(8,128)S(1)}, u32[]{:S(2)}, u32[]{:S(2)}) collective-permute-start(f32[5,8,128]{2,1,0:T(8,128)S(1)} %add.327), channel_id=1, source_target_pairs={{0,1},{1,2},{2,3},{3,4},{4,5},{5,6},{6,7},{7,8},{8,9},{9,10},{10,1... | collective-permute-start | bytes 61448 | tf_op jit(solution)/shard_map/while/body/eval_jaxpr/ppermute | solution.py:12
  232.3 9.0 %collective-permute-start.2 = (f32[5,8,128]{2,1,0:T(8,128)S(1)}, f32[5,8,128]{2,1,0:T(8,128)S(1)}, u32[]{:S(2)}, u32[]{:S(2)}) collective-permute-start(f32[5,8,128]{2,1,0:T(8,128)S(1)} %add.327), channel_id=1, source_target_pairs={{0,1},{1,2},{2,3},{3,4},{4,5},{5,6},{6,7},{7,8},{8,9},{9,10},{10,1... | collective-permute-start | bytes 61448 | tf_op jit(solution)/shard_map/while/body/eval_jaxpr/ppermute | solution.py:12
  241.3 9.0 %collective-permute-start.2 = (f32[5,8,128]{2,1,0:T(8,128)S(1)}, f32[5,8,128]{2,1,0:T(8,128)S(1)}, u32[]{:S(2)}, u32[]{:S(2)}) collective-permute-start(f32[5,8,128]{2,1,0:T(8,128)S(1)} %add.327), channel_id=1, source_target_pairs={{0,1},{1,2},{2,3},{3,4},{4,5},{5,6},{6,7},{7,8},{8,9},{9,10},{10,1... | collective-permute-start | bytes 61448 | tf_op jit(solution)/shard_map/while/body/eval_jaxpr/ppermute | solution.py:12
  250.3 9.0 %collective-permute-start.2 = (f32[5,8,128]{2,1,0:T(8,128)S(1)}, f32[5,8,128]{2,1,0:T(8,128)S(1)}, u32[]{:S(2)}, u32[]{:S(2)}) collective-permute-start(f32[5,8,128]{2,1,0:T(8,128)S(1)} %add.327), channel_id=1, source_target_pairs={{0,1},{1,2},{2,3},{3,4},{4,5},{5,6},{6,7},{7,8},{8,9},{9,10},{10,1... | collective-permute-start | bytes 61448 | tf_op jit(solution)/shard_map/while/body/eval_jaxpr/ppermute | solution.py:12
  259.4 9.0 %collective-permute-start.2 = (f32[5,8,128]{2,1,0:T(8,128)S(1)}, f32[5,8,128]{2,1,0:T(8,128)S(1)}, u32[]{:S(2)}, u32[]{:S(2)}) collective-permute-start(f32[5,8,128]{2,1,0:T(8,128)S(1)} %add.327), channel_id=1, source_target_pairs={{0,1},{1,2},{2,3},{3,4},{4,5},{5,6},{6,7},{7,8},{8,9},{9,10},{10,1... | collective-permute-start | bytes 61448 | tf_op jit(solution)/shard_map/while/body/eval_jaxpr/ppermute | solution.py:12
  268.4 9.0 %collective-permute-start.2 = (f32[5,8,128]{2,1,0:T(8,128)S(1)}, f32[5,8,128]{2,1,0:T(8,128)S(1)}, u32[]{:S(2)}, u32[]{:S(2)}) collective-permute-start(f32[5,8,128]{2,1,0:T(8,128)S(1)} %add.327), channel_id=1, source_target_pairs={{0,1},{1,2},{2,3},{3,4},{4,5},{5,6},{6,7},{7,8},{8,9},{9,10},{10,1... | collective-permute-start | bytes 61448 | tf_op jit(solution)/shard_map/while/body/eval_jaxpr/ppermute | solution.py:12
  277.4 9.0 %collective-permute-start.2 = (f32[5,8,128]{2,1,0:T(8,128)S(1)}, f32[5,8,128]{2,1,0:T(8,128)S(1)}, u32[]{:S(2)}, u32[]{:S(2)}) collective-permute-start(f32[5,8,128]{2,1,0:T(8,128)S(1)} %add.327), channel_id=1, source_target_pairs={{0,1},{1,2},{2,3},{3,4},{4,5},{5,6},{6,7},{7,8},{8,9},{9,10},{10,1... | collective-permute-start | bytes 61448 | tf_op jit(solution)/shard_map/while/body/eval_jaxpr/ppermute | solution.py:12
  286.4 9.1 %collective-permute-start.2 = (f32[5,8,128]{2,1,0:T(8,128)S(1)}, f32[5,8,128]{2,1,0:T(8,128)S(1)}, u32[]{:S(2)}, u32[]{:S(2)}) collective-permute-start(f32[5,8,128]{2,1,0:T(8,128)S(1)} %add.327), channel_id=1, source_target_pairs={{0,1},{1,2},{2,3},{3,4},{4,5},{5,6},{6,7},{7,8},{8,9},{9,10},{10,1... | collective-permute-start | bytes 61448 | tf_op jit(solution)/shard_map/while/body/eval_jaxpr/ppermute | solution.py:12
  295.5 9.0 %collective-permute-start.2 = (f32[5,8,128]{2,1,0:T(8,128)S(1)}, f32[5,8,128]{2,1,0:T(8,128)S(1)}, u32[]{:S(2)}, u32[]{:S(2)}) collective-permute-start(f32[5,8,128]{2,1,0:T(8,128)S(1)} %add.327), channel_id=1, source_target_pairs={{0,1},{1,2},{2,3},{3,4},{4,5},{5,6},{6,7},{7,8},{8,9},{9,10},{10,1... | collective-permute-start | bytes 61448 | tf_op jit(solution)/shard_map/while/body/eval_jaxpr/ppermute | solution.py:12
  304.6 9.0 %collective-permute-start.2 = (f32[5,8,128]{2,1,0:T(8,128)S(1)}, f32[5,8,128]{2,1,0:T(8,128)S(1)}, u32[]{:S(2)}, u32[]{:S(2)}) collective-permute-start(f32[5,8,128]{2,1,0:T(8,128)S(1)} %add.327), channel_id=1, source_target_pairs={{0,1},{1,2},{2,3},{3,4},{4,5},{5,6},{6,7},{7,8},{8,9},{9,10},{10,1... | collective-permute-start | bytes 61448 | tf_op jit(solution)/shard_map/while/body/eval_jaxpr/ppermute | solution.py:12
  313.6 9.0 %collective-permute-start.2 = (f32[5,8,128]{2,1,0:T(8,128)S(1)}, f32[5,8,128]{2,1,0:T(8,128)S(1)}, u32[]{:S(2)}, u32[]{:S(2)}) collective-permute-start(f32[5,8,128]{2,1,0:T(8,128)S(1)} %add.327), channel_id=1, source_target_pairs={{0,1},{1,2},{2,3},{3,4},{4,5},{5,6},{6,7},{7,8},{8,9},{9,10},{10,1... | collective-permute-start | bytes 61448 | tf_op jit(solution)/shard_map/while/body/eval_jaxpr/ppermute | solution.py:12
  322.6 9.0 %collective-permute-start.2 = (f32[5,8,128]{2,1,0:T(8,128)S(1)}, f32[5,8,128]{2,1,0:T(8,128)S(1)}, u32[]{:S(2)}, u32[]{:S(2)}) collective-permute-start(f32[5,8,128]{2,1,0:T(8,128)S(1)} %add.327), channel_id=1, source_target_pairs={{0,1},{1,2},{2,3},{3,4},{4,5},{5,6},{6,7},{7,8},{8,9},{9,10},{10,1... | collective-permute-start | bytes 61448 | tf_op jit(solution)/shard_map/while/body/eval_jaxpr/ppermute | solution.py:12
  331.6 9.0 %collective-permute-start.2 = (f32[5,8,128]{2,1,0:T(8,128)S(1)}, f32[5,8,128]{2,1,0:T(8,128)S(1)}, u32[]{:S(2)}, u32[]{:S(2)}) collective-permute-start(f32[5,8,128]{2,1,0:T(8,128)S(1)} %add.327), channel_id=1, source_target_pairs={{0,1},{1,2},{2,3},{3,4},{4,5},{5,6},{6,7},{7,8},{8,9},{9,10},{10,1... | collective-permute-start | bytes 61448 | tf_op jit(solution)/shard_map/while/body/eval_jaxpr/ppermute | solution.py:12
  340.7 9.0 %collective-permute-start.2 = (f32[5,8,128]{2,1,0:T(8,128)S(1)}, f32[5,8,128]{2,1,0:T(8,128)S(1)}, u32[]{:S(2)}, u32[]{:S(2)}) collective-permute-start(f32[5,8,128]{2,1,0:T(8,128)S(1)} %add.327), channel_id=1, source_target_pairs={{0,1},{1,2},{2,3},{3,4},{4,5},{5,6},{6,7},{7,8},{8,9},{9,10},{10,1... | collective-permute-start | bytes 61448 | tf_op jit(solution)/shard_map/while/body/eval_jaxpr/ppermute | solution.py:12
  349.7 9.1 %collective-permute-start.2 = (f32[5,8,128]{2,1,0:T(8,128)S(1)}, f32[5,8,128]{2,1,0:T(8,128)S(1)}, u32[]{:S(2)}, u32[]{:S(2)}) collective-permute-start(f32[5,8,128]{2,1,0:T(8,128)S(1)} %add.327), channel_id=1, source_target_pairs={{0,1},{1,2},{2,3},{3,4},{4,5},{5,6},{6,7},{7,8},{8,9},{9,10},{10,1... | collective-permute-start | bytes 61448 | tf_op jit(solution)/shard_map/while/body/eval_jaxpr/ppermute | solution.py:12
  358.8 9.0 %collective-permute-start.2 = (f32[5,8,128]{2,1,0:T(8,128)S(1)}, f32[5,8,128]{2,1,0:T(8,128)S(1)}, u32[]{:S(2)}, u32[]{:S(2)}) collective-permute-start(f32[5,8,128]{2,1,0:T(8,128)S(1)} %add.327), channel_id=1, source_target_pairs={{0,1},{1,2},{2,3},{3,4},{4,5},{5,6},{6,7},{7,8},{8,9},{9,10},{10,1... | collective-permute-start | bytes 61448 | tf_op jit(solution)/shard_map/while/body/eval_jaxpr/ppermute | solution.py:12
  367.8 9.0 %collective-permute-start.2 = (f32[5,8,128]{2,1,0:T(8,128)S(1)}, f32[5,8,128]{2,1,0:T(8,128)S(1)}, u32[]{:S(2)}, u32[]{:S(2)}) collective-permute-start(f32[5,8,128]{2,1,0:T(8,128)S(1)} %add.327), channel_id=1, source_target_pairs={{0,1},{1,2},{2,3},{3,4},{4,5},{5,6},{6,7},{7,8},{8,9},{9,10},{10,1... | collective-permute-start | bytes 61448 | tf_op jit(solution)/shard_map/while/body/eval_jaxpr/ppermute | solution.py:12
  376.8 9.0 %collective-permute-start.2 = (f32[5,8,128]{2,1,0:T(8,128)S(1)}, f32[5,8,128]{2,1,0:T(8,128)S(1)}, u32[]{:S(2)}, u32[]{:S(2)}) collective-permute-start(f32[5,8,128]{2,1,0:T(8,128)S(1)} %add.327), channel_id=1, source_target_pairs={{0,1},{1,2},{2,3},{3,4},{4,5},{5,6},{6,7},{7,8},{8,9},{9,10},{10,1... | collective-permute-start | bytes 61448 | tf_op jit(solution)/shard_map/while/body/eval_jaxpr/ppermute | solution.py:12
  385.9 9.0 %collective-permute-start.2 = (f32[5,8,128]{2,1,0:T(8,128)S(1)}, f32[5,8,128]{2,1,0:T(8,128)S(1)}, u32[]{:S(2)}, u32[]{:S(2)}) collective-permute-start(f32[5,8,128]{2,1,0:T(8,128)S(1)} %add.327), channel_id=1, source_target_pairs={{0,1},{1,2},{2,3},{3,4},{4,5},{5,6},{6,7},{7,8},{8,9},{9,10},{10,1... | collective-permute-start | bytes 61448 | tf_op jit(solution)/shard_map/while/body/eval_jaxpr/ppermute | solution.py:12
  394.9 9.0 %collective-permute-start.2 = (f32[5,8,128]{2,1,0:T(8,128)S(1)}, f32[5,8,128]{2,1,0:T(8,128)S(1)}, u32[]{:S(2)}, u32[]{:S(2)}) collective-permute-start(f32[5,8,128]{2,1,0:T(8,128)S(1)} %add.327), channel_id=1, source_target_pairs={{0,1},{1,2},{2,3},{3,4},{4,5},{5,6},{6,7},{7,8},{8,9},{9,10},{10,1... | collective-permute-start | bytes 61448 | tf_op jit(solution)/shard_map/while/body/eval_jaxpr/ppermute | solution.py:12
  403.9 9.0 %collective-permute-start.2 = (f32[5,8,128]{2,1,0:T(8,128)S(1)}, f32[5,8,128]{2,1,0:T(8,128)S(1)}, u32[]{:S(2)}, u32[]{:S(2)}) collective-permute-start(f32[5,8,128]{2,1,0:T(8,128)S(1)} %add.327), channel_id=1, source_target_pairs={{0,1},{1,2},{2,3},{3,4},{4,5},{5,6},{6,7},{7,8},{8,9},{9,10},{10,1... | collective-permute-start | bytes 61448 | tf_op jit(solution)/shard_map/while/body/eval_jaxpr/ppermute | solution.py:12
  412.9 9.0 %collective-permute-start.2 = (f32[5,8,128]{2,1,0:T(8,128)S(1)}, f32[5,8,128]{2,1,0:T(8,128)S(1)}, u32[]{:S(2)}, u32[]{:S(2)}) collective-permute-start(f32[5,8,128]{2,1,0:T(8,128)S(1)} %add.327), channel_id=1, source_target_pairs={{0,1},{1,2},{2,3},{3,4},{4,5},{5,6},{6,7},{7,8},{8,9},{9,10},{10,1... | collective-permute-start | bytes 61448 | tf_op jit(solution)/shard_map/while/body/eval_jaxpr/ppermute | solution.py:12
  422.0 9.0 %collective-permute-start.2 = (f32[5,8,128]{2,1,0:T(8,128)S(1)}, f32[5,8,128]{2,1,0:T(8,128)S(1)}, u32[]{:S(2)}, u32[]{:S(2)}) collective-permute-start(f32[5,8,128]{2,1,0:T(8,128)S(1)} %add.327), channel_id=1, source_target_pairs={{0,1},{1,2},{2,3},{3,4},{4,5},{5,6},{6,7},{7,8},{8,9},{9,10},{10,1... | collective-permute-start | bytes 61448 | tf_op jit(solution)/shard_map/while/body/eval_jaxpr/ppermute | solution.py:12
  476.3 9.3 %collective-permute-start.3 = (f32[5,8,128]{2,1,0:T(8,128)S(1)}, f32[5,8,128]{2,1,0:T(8,128)S(1)}, u32[]{:S(2)}, u32[]{:S(2)}) collective-permute-start(f32[5,8,128]{2,1,0:T(8,128)S(1)} %add.330), channel_id=1, source_target_pairs={{1,0},{2,1},{3,2},{4,3},{5,4},{6,5},{7,6},{8,7},{9,8},{10,9},{11,1... | collective-permute-start | bytes 61448 | tf_op jit(solution)/shard_map/while/body/eval_jaxpr/ppermute | solution.py:12
  485.6 9.0 %collective-permute-start.3 = (f32[5,8,128]{2,1,0:T(8,128)S(1)}, f32[5,8,128]{2,1,0:T(8,128)S(1)}, u32[]{:S(2)}, u32[]{:S(2)}) collective-permute-start(f32[5,8,128]{2,1,0:T(8,128)S(1)} %add.330), channel_id=1, source_target_pairs={{1,0},{2,1},{3,2},{4,3},{5,4},{6,5},{7,6},{8,7},{9,8},{10,9},{11,1... | collective-permute-start | bytes 61448 | tf_op jit(solution)/shard_map/while/body/eval_jaxpr/ppermute | solution.py:12
  494.6 9.0 %collective-permute-start.3 = (f32[5,8,128]{2,1,0:T(8,128)S(1)}, f32[5,8,128]{2,1,0:T(8,128)S(1)}, u32[]{:S(2)}, u32[]{:S(2)}) collective-permute-start(f32[5,8,128]{2,1,0:T(8,128)S(1)} %add.330), channel_id=1, source_target_pairs={{1,0},{2,1},{3,2},{4,3},{5,4},{6,5},{7,6},{8,7},{9,8},{10,9},{11,1... | collective-permute-start | bytes 61448 | tf_op jit(solution)/shard_map/while/body/eval_jaxpr/ppermute | solution.py:12
  503.6 9.0 %collective-permute-start.3 = (f32[5,8,128]{2,1,0:T(8,128)S(1)}, f32[5,8,128]{2,1,0:T(8,128)S(1)}, u32[]{:S(2)}, u32[]{:S(2)}) collective-permute-start(f32[5,8,128]{2,1,0:T(8,128)S(1)} %add.330), channel_id=1, source_target_pairs={{1,0},{2,1},{3,2},{4,3},{5,4},{6,5},{7,6},{8,7},{9,8},{10,9},{11,1... | collective-permute-start | bytes 61448 | tf_op jit(solution)/shard_map/while/body/eval_jaxpr/ppermute | solution.py:12
  521.7 9.0 %collective-permute-start.3 = (f32[5,8,128]{2,1,0:T(8,128)S(1)}, f32[5,8,128]{2,1,0:T(8,128)S(1)}, u32[]{:S(2)}, u32[]{:S(2)}) collective-permute-start(f32[5,8,128]{2,1,0:T(8,128)S(1)} %add.330), channel_id=1, source_target_pairs={{1,0},{2,1},{3,2},{4,3},{5,4},{6,5},{7,6},{8,7},{9,8},{10,9},{11,1... | collective-permute-start | bytes 61448 | tf_op jit(solution)/shard_map/while/body/eval_jaxpr/ppermute | solution.py:12
  530.7 9.0 %collective-permute-start.3 = (f32[5,8,128]{2,1,0:T(8,128)S(1)}, f32[5,8,128]{2,1,0:T(8,128)S(1)}, u32[]{:S(2)}, u32[]{:S(2)}) collective-permute-start(f32[5,8,128]{2,1,0:T(8,128)S(1)} %add.330), channel_id=1, source_target_pairs={{1,0},{2,1},{3,2},{4,3},{5,4},{6,5},{7,6},{8,7},{9,8},{10,9},{11,1... | collective-permute-start | bytes 61448 | tf_op jit(solution)/shard_map/while/body/eval_jaxpr/ppermute | solution.py:12
  539.7 9.0 %collective-permute-start.3 = (f32[5,8,128]{2,1,0:T(8,128)S(1)}, f32[5,8,128]{2,1,0:T(8,128)S(1)}, u32[]{:S(2)}, u32[]{:S(2)}) collective-permute-start(f32[5,8,128]{2,1,0:T(8,128)S(1)} %add.330), channel_id=1, source_target_pairs={{1,0},{2,1},{3,2},{4,3},{5,4},{6,5},{7,6},{8,7},{9,8},{10,9},{11,1... | collective-permute-start | bytes 61448 | tf_op jit(solution)/shard_map/while/body/eval_jaxpr/ppermute | solution.py:12
  548.8 9.0 %collective-permute-start.3 = (f32[5,8,128]{2,1,0:T(8,128)S(1)}, f32[5,8,128]{2,1,0:T(8,128)S(1)}, u32[]{:S(2)}, u32[]{:S(2)}) collective-permute-start(f32[5,8,128]{2,1,0:T(8,128)S(1)} %add.330), channel_id=1, source_target_pairs={{1,0},{2,1},{3,2},{4,3},{5,4},{6,5},{7,6},{8,7},{9,8},{10,9},{11,1... | collective-permute-start | bytes 61448 | tf_op jit(solution)/shard_map/while/body/eval_jaxpr/ppermute | solution.py:12
  566.8 9.0 %collective-permute-start.3 = (f32[5,8,128]{2,1,0:T(8,128)S(1)}, f32[5,8,128]{2,1,0:T(8,128)S(1)}, u32[]{:S(2)}, u32[]{:S(2)}) collective-permute-start(f32[5,8,128]{2,1,0:T(8,128)S(1)} %add.330), channel_id=1, source_target_pairs={{1,0},{2,1},{3,2},{4,3},{5,4},{6,5},{7,6},{8,7},{9,8},{10,9},{11,1... | collective-permute-start | bytes 61448 | tf_op jit(solution)/shard_map/while/body/eval_jaxpr/ppermute | solution.py:12
  575.8 9.1 %collective-permute-start.3 = (f32[5,8,128]{2,1,0:T(8,128)S(1)}, f32[5,8,128]{2,1,0:T(8,128)S(1)}, u32[]{:S(2)}, u32[]{:S(2)}) collective-permute-start(f32[5,8,128]{2,1,0:T(8,128)S(1)} %add.330), channel_id=1, source_target_pairs={{1,0},{2,1},{3,2},{4,3},{5,4},{6,5},{7,6},{8,7},{9,8},{10,9},{11,1... | collective-permute-start | bytes 61448 | tf_op jit(solution)/shard_map/while/body/eval_jaxpr/ppermute | solution.py:12
  594.0 9.0 %collective-permute-start.3 = (f32[5,8,128]{2,1,0:T(8,128)S(1)}, f32[5,8,128]{2,1,0:T(8,128)S(1)}, u32[]{:S(2)}, u32[]{:S(2)}) collective-permute-start(f32[5,8,128]{2,1,0:T(8,128)S(1)} %add.330), channel_id=1, source_target_pairs={{1,0},{2,1},{3,2},{4,3},{5,4},{6,5},{7,6},{8,7},{9,8},{10,9},{11,1... | collective-permute-start | bytes 61448 | tf_op jit(solution)/shard_map/while/body/eval_jaxpr/ppermute | solution.py:12
  603.0 9.0 %collective-permute-start.3 = (f32[5,8,128]{2,1,0:T(8,128)S(1)}, f32[5,8,128]{2,1,0:T(8,128)S(1)}, u32[]{:S(2)}, u32[]{:S(2)}) collective-permute-start(f32[5,8,128]{2,1,0:T(8,128)S(1)} %add.330), channel_id=1, source_target_pairs={{1,0},{2,1},{3,2},{4,3},{5,4},{6,5},{7,6},{8,7},{9,8},{10,9},{11,1... | collective-permute-start | bytes 61448 | tf_op jit(solution)/shard_map/while/body/eval_jaxpr/ppermute | solution.py:12
  612.0 9.0 %collective-permute-start.3 = (f32[5,8,128]{2,1,0:T(8,128)S(1)}, f32[5,8,128]{2,1,0:T(8,128)S(1)}, u32[]{:S(2)}, u32[]{:S(2)}) collective-permute-start(f32[5,8,128]{2,1,0:T(8,128)S(1)} %add.330), channel_id=1, source_target_pairs={{1,0},{2,1},{3,2},{4,3},{5,4},{6,5},{7,6},{8,7},{9,8},{10,9},{11,1... | collective-permute-start | bytes 61448 | tf_op jit(solution)/shard_map/while/body/eval_jaxpr/ppermute | solution.py:12
  621.0 9.0 %collective-permute-start.3 = (f32[5,8,128]{2,1,0:T(8,128)S(1)}, f32[5,8,128]{2,1,0:T(8,128)S(1)}, u32[]{:S(2)}, u32[]{:S(2)}) collective-permute-start(f32[5,8,128]{2,1,0:T(8,128)S(1)} %add.330), channel_id=1, source_target_pairs={{1,0},{2,1},{3,2},{4,3},{5,4},{6,5},{7,6},{8,7},{9,8},{10,9},{11,1... | collective-permute-start | bytes 61448 | tf_op jit(solution)/shard_map/while/body/eval_jaxpr/ppermute | solution.py:12
  639.1 9.1 %collective-permute-start.3 = (f32[5,8,128]{2,1,0:T(8,128)S(1)}, f32[5,8,128]{2,1,0:T(8,128)S(1)}, u32[]{:S(2)}, u32[]{:S(2)}) collective-permute-start(f32[5,8,128]{2,1,0:T(8,128)S(1)} %add.330), channel_id=1, source_target_pairs={{1,0},{2,1},{3,2},{4,3},{5,4},{6,5},{7,6},{8,7},{9,8},{10,9},{11,1... | collective-permute-start | bytes 61448 | tf_op jit(solution)/shard_map/while/body/eval_jaxpr/ppermute | solution.py:12
  648.2 9.0 %collective-permute-start.3 = (f32[5,8,128]{2,1,0:T(8,128)S(1)}, f32[5,8,128]{2,1,0:T(8,128)S(1)}, u32[]{:S(2)}, u32[]{:S(2)}) collective-permute-start(f32[5,8,128]{2,1,0:T(8,128)S(1)} %add.330), channel_id=1, source_target_pairs={{1,0},{2,1},{3,2},{4,3},{5,4},{6,5},{7,6},{8,7},{9,8},{10,9},{11,1... | collective-permute-start | bytes 61448 | tf_op jit(solution)/shard_map/while/body/eval_jaxpr/ppermute | solution.py:12
  657.2 9.0 %collective-permute-start.3 = (f32[5,8,128]{2,1,0:T(8,128)S(1)}, f32[5,8,128]{2,1,0:T(8,128)S(1)}, u32[]{:S(2)}, u32[]{:S(2)}) collective-permute-start(f32[5,8,128]{2,1,0:T(8,128)S(1)} %add.330), channel_id=1, source_target_pairs={{1,0},{2,1},{3,2},{4,3},{5,4},{6,5},{7,6},{8,7},{9,8},{10,9},{11,1... | collective-permute-start | bytes 61448 | tf_op jit(solution)/shard_map/while/body/eval_jaxpr/ppermute | solution.py:12
  675.3 9.0 %collective-permute-start.3 = (f32[5,8,128]{2,1,0:T(8,128)S(1)}, f32[5,8,128]{2,1,0:T(8,128)S(1)}, u32[]{:S(2)}, u32[]{:S(2)}) collective-permute-start(f32[5,8,128]{2,1,0:T(8,128)S(1)} %add.330), channel_id=1, source_target_pairs={{1,0},{2,1},{3,2},{4,3},{5,4},{6,5},{7,6},{8,7},{9,8},{10,9},{11,1... | collective-permute-start | bytes 61448 | tf_op jit(solution)/shard_map/while/body/eval_jaxpr/ppermute | solution.py:12
  (36 other events, 315.7 us)
where the time goes:
time: 786 us; the launch traced here: 780 us
  starting transfers between devices  335 us (43%)
  waiting for transfers between devices  311 us (40%)
  local copies, waits for them, and re-layouts  86.3 us (11%)
  other arithmetic  40.4 us (5%)
    ppermute x76, starting transfers between devices, from_behind(): lax.ppermute(value, axis, [(source, source + steps) for source in range(f...  323 us
    ppermute x76, waiting for transfers between devices, from_behind(): lax.ppermute(value, axis, [(source, source + steps) for source in range(f...  302 us
    dynamic_slice x32, local copies, waits for them, and re-layouts, run_advance(): here = lax.dynamic_index_in_dim(coupling, k, line_axis + 1, keepdims=False)  39.2 us
    dynamic_slice x32, local copies, waits for them, and re-layouts, compose_advance(): here = lax.dynamic_index_in_dim(coupling, k, line_axis + 1, keepdims=False)  39.2 us
    reduce_sum x174, other arithmetic, apply_block(): return jnp.sum(blocks * vector[None], axis=1)  33.1 us
  transfers between devices with their start and end apart: 80, of which 80 were waited for; matrix products, arithmetic and copies ran while one was open for 0% of the time, Pallas kernels for 0%

commit v1 on v0

v1 whole, which is shorter than its diff:
```python
import jax
import jax.numpy as jnp
from jax import lax
from jax.experimental import pallas as pl
from jax.experimental.pallas import tpu as pltpu
from jax.sharding import PartitionSpec as P

DISSIPATION = 0.1
MESH = pl.DeviceIdType.MESH
F32 = jnp.float32

V = 5
E = V * V
NPX, NPY, NPZ = 8, 32, 8
IN_Z = NPY // NPZ
CX, CY = 8, 16
ROWS = CX * CY
XM, YM = 76, 80
XV, YV = 12, 16
XO = CY // NPX


def block(ref, rows):
    return ref[:, rows, :].reshape(V, V, 8, 128)


def total(terms):
    while len(terms) > 1:
        terms = [terms[k] + terms[k + 1] if k + 1 < len(terms) else terms[k] for k in range(0, len(terms), 2)]
    return terms[0]


def apply(m, x):
    return total([m[:, c] * x[c][None] for c in range(V)])


def product(m, b):
    rows = [total([m[a, c][None] * b[c] for c in range(V)]) for a in range(V)]
    return jnp.stack(rows)


def device_products(lo, up, n, rows, psi, emit):
    first = block(lo, rows(0))
    psi[0] = first

    def forward(i, m):
        m = product(block(lo, rows(i)), m)
        psi[i] = m
        return m

    last = lax.fori_loop(1, n, forward, first)
    emit(0, last)

    def backward(t, z):
        i = n - 2 - t
        return psi[i] + product(block(up, rows(i)), z)

    emit(E, lax.fori_loop(0, n - 1, backward, last))

    def upward(t, m):
        return product(block(up, rows(n - 2 - t)), m)

    emit(2 * E, lax.fori_loop(0, n - 1, upward, block(up, rows(n - 1))))


def forward_cells(source, lo, rows, n, start, save):
    def step(i, carry):
        out = []
        for t, f in enumerate(carry):
            cur = source(i, t)
            if f is not None:
                cur = cur - apply(block(lo, rows(i, t)), f)
            save(i, t, cur)
            out.append(cur)
        return tuple(out)

    begin = 0
    if start[0] is None:
        start, begin = step(0, start), 1
    return lax.fori_loop(begin, n, step, start)


def backward_cells(source, up, rows, n, start, save):
    def step(k, carry):
        i = n - 1 - k
        out = []
        for t, g in enumerate(carry):
            cur = source(i, t)
            if g is not None:
                cur = cur - apply(block(up, rows(i, t)), g)
            if save is not None:
                save(i, t, cur)
            out.append(cur)
        return tuple(out)

    begin = 0
    if start[0] is None:
        start, begin = step(0, start), 1
    return lax.fori_loop(begin, n, step, start)


def kernel(field, forcing, xi, xl, xu, yi, yl, yu, out,
           fx, fo, xi_v, xl_v, xu_v, yi_v, yl_v, yu_v, res,
           fy, hx, hy, rhs, psi, sx, fwx, sy, fwy,
           xm_out, xm_in, xv_out, xv_in, xr_out, xr_in,
           ym_out, ym_in, yv_out, yv_in, yr_out, yr_in, xmat, ymat, cmat,
           load_s, halo_ss, halo_rs, xm_ss, xm_rs, xv_ss, xv_rs, xr_ss, xr_rs,
           ym_ss, ym_rs, yv_ss, yv_rs, yr_ss, yr_rs, out_s):
    px, py = lax.axis_index("px"), lax.axis_index("py")
    core, z = lax.rem(px, 2), lax.div(py, IN_Z)

    def owner_of(r):
        return IN_Z * r + lax.rem(2 * core + r, IN_Z)

    is_owner = py == owner_of(z)

    barrier = pltpu.get_barrier_semaphore()

    def greet_x(k, _):
        pl.semaphore_signal(barrier, inc=1, device_id=(lax.rem(px + k, NPX), py), device_id_type=MESH)
        return 0

    def greet_y(k, _):
        pl.semaphore_signal(barrier, inc=1, device_id=(px, lax.rem(py + k, NPY)), device_id_type=MESH)
        return 0

    lax.fori_loop(1, NPX, greet_x, 0)
    lax.fori_loop(1, NPY, greet_y, 0)

    mine = slice(2 * CY, 2 * CY + ROWS)
    loads = [
        pltpu.make_async_copy(a, b, load_s.at[k])
        for k, (a, b) in enumerate([
            (field, fx.at[:, mine, :]), (xl, xl_v), (xu, xu_v), (yl, yl_v), (yu, yu_v),
            (forcing, fo), (xi, xi_v), (yi, yi_v)])
    ]
    for c in loads:
        c.start()
    in_field, in_xl, in_xu, in_yl, in_yu, in_fo, in_xi, in_yi = loads

    def x_rows(i, h):
        return pl.ds(pl.multiple_of(CY * i + 8 * h, 8), 8)

    def y_rows(j, _=0):
        return pl.ds(j, 8, stride=CY)

    in_field.wait()

    def turn(j, _):
        fy[2 + j] = fx[:, pl.ds(2 * CY + j, 8, stride=CY), :]
        return 0

    lax.fori_loop(0, CY, turn, 0)

    in_xl.wait()
    in_xu.wait()
    for h in range(2):
        def emit(base, m, h=h):
            for e in range(E):
                xm_out[pl.ds(8 * h * XM + base + e, 8, stride=XM), :] = m[e // V, e % V]

        device_products(xl_v, xu_v, CX, lambda i, h=h: x_rows(i, h), psi, emit)

    pl.semaphore_wait(barrier, NPX + NPY - 2)

    right, left = lax.rem(px + 1, NPX), lax.rem(px + NPX - 1, NPX)
    north, south = lax.rem(py + 1, NPY), lax.rem(py + NPY - 1, NPY)
    halos = [
        pltpu.make_async_remote_copy(a, b, halo_ss.at[k], halo_rs.at[k], device_id=d, device_id_type=MESH)
        for k, (a, b, d) in enumerate([
            (fx.at[:, ROWS : ROWS + 2 * CY, :], hx.at[0], (right, py)),
            (fx.at[:, 2 * CY : 4 * CY, :], hx.at[1], (left, py)),
            (fy.at[CY : CY + 2], hy.at[0], (px, north)),
            (fy.at[2:4], hy.at[1], (px, south))])
    ]
    for c in halos:
        c.start()

    def at(ref, k, size):
        return ref.at[pl.ds(pl.multiple_of(k * size, 8), size), :]

    def x_copy(src, dst, ss, rs, size, k):
        return pltpu.make_async_remote_copy(
            at(src, k, size), at(dst, px, size), ss.at[k], rs.at[px], device_id=(k, py), device_id_type=MESH)

    def x_send(src, dst, ss, rs, size):
        pltpu.make_async_copy(at(src, px, size), at(dst, px, size), rs.at[px]).start()

        def one(k, _):
            x_copy(src, dst, ss, rs, size, lax.rem(px + k, NPX)).start()
            return 0

        lax.fori_loop(1, NPX, one, 0)

    def x_sent(src, dst, ss, rs, size):
        def one(k, _):
            x_copy(src, dst, ss, rs, size, lax.rem(px + k, NPX)).wait_send()
            return 0

        lax.fori_loop(1, NPX, one, 0)

    def received(dst, rs, size, count):
        def one(k, _):
            pltpu.make_async_copy(at(dst, k, size), at(dst, k, size), rs.at[k]).wait()
            return 0

        lax.fori_loop(0, count, one, 0)

    def y_copy(src, dst, ss, rs, size, r):
        return pltpu.make_async_remote_copy(
            at(src, r, size), at(dst, py, size), ss.at[r], rs.at[py], device_id=(px, owner_of(r)), device_id_type=MESH)

    def y_send(src, dst, ss, rs, size):
        @pl.when(is_owner)
        def _():
            pltpu.make_async_copy(at(src, z, size), at(dst, py, size), rs.at[py]).start()

        @pl.when(jnp.logical_not(is_owner))
        def _():
            y_copy(src, dst, ss, rs, size, z).start()

        def one(k, _):
            y_copy(src, dst, ss, rs, size, lax.rem(z + k, NPZ)).start()
            return 0

        lax.fori_loop(1, NPZ, one, 0)

    def y_sent(src, dst, ss, rs, size):
        @pl.when(jnp.logical_not(is_owner))
        def _():
            y_copy(src, dst, ss, rs, size, z).wait_send()

        def one(k, _):
            y_copy(src, dst, ss, rs, size, lax.rem(z + k, NPZ)).wait_send()
            return 0

        lax.fori_loop(1, NPZ, one, 0)

    xm = (xm_out, xm_in, xm_ss, xm_rs, XO * XM)
    xv = (xv_out, xv_in, xv_ss, xv_rs, XO * XV)
    xr = (xr_out, xr_in, xr_ss, xr_rs, XO * XV)
    ym = (ym_out, ym_in, ym_ss, ym_rs, YM)
    yv = (yv_out, yv_in, yv_ss, yv_rs, YV)
    x_send(*xm)

    in_yl.wait()
    in_yu.wait()

    def emit_y(base, m):
        for e in range(E):
            ym_out[pl.ds(base + e, 8, stride=YM), :] = m[e // V, e % V]

    device_products(yl_v, yu_v, CY, y_rows, psi, emit_y)
    y_send(*ym)

    in_fo.wait()
    for c in halos:
        c.wait()
    fx[:, 0 : 2 * CY, :] = jnp.where(px == 0, 0.0, hx[0])
    fx[:, 2 * CY + ROWS :, :] = jnp.where(px == NPX - 1, 0.0, hx[1])
    fy[0:2] = jnp.where(py == 0, 0.0, hy[0])
    fy[CY + 2 :] = jnp.where(py == NPY - 1, 0.0, hy[1])

    def difference(v):
        return v[0] - 4.0 * v[1] + 6.0 * v[2] - 4.0 * v[3] + v[4]

    def along_y(j, _):
        d = difference([fy[j + k] for k in range(5)])
        rhs[:, y_rows(j), :] = fo[:, y_rows(j), :] - DISSIPATION * d
        return 0

    lax.fori_loop(0, CY, along_y, 0)
    in_xi.wait()

    def x_source(i, h):
        d = difference([fx[:, x_rows(i + k, h), :] for k in range(5)])
        s = apply(block(xi_v, x_rows(i, h)), rhs[:, x_rows(i, h), :] - DISSIPATION * d)
        sx[:, x_rows(i, h), :] = s
        return s

    def save_fwx(i, h, f):
        fwx[:, x_rows(i, h), :] = f

    def load_fwx(i, h):
        return fwx[:, x_rows(i, h), :]

    ends = forward_cells(x_source, xl_v, x_rows, CX, (None, None), save_fwx)
    starts = backward_cells(load_fwx, xu_v, x_rows, CX, (None, None), None)
    for h in range(2):
        for c in range(V):
            xv_out[pl.ds(8 * h * XV + c, 8, stride=XV), :] = ends[h][c]
            xv_out[pl.ds(8 * h * XV + V + c, 8, stride=XV), :] = starts[h][c]
    x_send(*xv)

    place = lax.broadcasted_iota(jnp.int32, (V, 8, 128), 1)

    def chain(m, v):
        def one(_, a):
            return tuple(jnp.where(place == 0, 0.0, pltpu.roll(vk + apply(mk(), ak), 1, axis=1))
                         for vk, mk, ak in zip(v, m, a))

        return lax.fori_loop(0, 7, one, tuple(jnp.zeros((V, 8, 128), F32) for _ in v))

    def chain_back(m, v):
        def one(_, b):
            return tuple(jnp.where(place == 7, 0.0, pltpu.roll(vk + apply(mk(), bk), 7, axis=1))
                         for vk, mk, bk in zip(v, m, b))

        return lax.fori_loop(0, 7, one, tuple(jnp.zeros((V, 8, 128), F32) for _ in v))

    def held(ref, *at_):
        return lambda: ref[at_].reshape(V, V, 8, 128)

    received(xm_in, xm_rs, XO * XM, NPX)
    for r in range(XO):
        for e in range(3 * E):
            xmat[r, e // E, e % E] = xm_in[pl.ds(r * XM + e, 8, stride=XO * XM), :]
    received(xv_in, xv_rs, XO * XV, NPX)

    def rows_of(ref, first, stride):
        return jnp.stack([ref[pl.ds(first + c, 8, stride=stride), :] for c in range(V)])

    v = [rows_of(xv_in, r * XV, XO * XV) for r in range(XO)]
    w = [rows_of(xv_in, r * XV + V, XO * XV) for r in range(XO)]
    a = chain([held(xmat, r, 0) for r in range(XO)], v)
    w = [w[r] - apply(held(xmat, r, 1)(), a[r]) for r in range(XO)]
    b = chain_back([held(xmat, r, 2) for r in range(XO)], w)
    for r in range(XO):
        for c in range(V):
            xr_out[pl.ds(r * XV + c, 8, stride=XO * XV), :] = a[r][c]
            xr_out[pl.ds(r * XV + V + c, 8, stride=XO * XV), :] = b[r][c]
    x_send(*xr)
    received(xr_in, xr_rs, XO * XV, NPX)

    before = tuple(rows_of(xr_in, 8 * h * XV, XV) for h in range(2))
    after = tuple(rows_of(xr_in, 8 * h * XV + V, XV) for h in range(2))

    def load_sx(i, h):
        return sx[:, x_rows(i, h), :]

    forward_cells(load_sx, xl_v, x_rows, CX, before, save_fwx)
    backward_cells(load_fwx, xu_v, x_rows, CX, after, save_fwx)

    in_yi.wait()

    def y_source(j, _):
        s = apply(block(yi_v, y_rows(j)), fwx[:, y_rows(j), :])
        sy[j] = s
        return s

    def save_fwy(j, _, f):
        fwy[j] = f

    def load_fwy(j, _):
        return fwy[j]

    end, = forward_cells(y_source, yl_v, y_rows, CY, (None,), save_fwy)
    start, = backward_cells(load_fwy, yu_v, y_rows, CY, (None,), None)
    for c in range(V):
        yv_out[pl.ds(c, 8, stride=YV), :] = end[c]
        yv_out[pl.ds(V + c, 8, stride=YV), :] = start[c]
    y_send(*yv)

    def y_back(d):
        return pltpu.make_async_remote_copy(
            at(yr_out, d, YV), at(yr_in, z, YV), yr_ss.at[d], yr_rs.at[z], device_id=(px, d), device_id_type=MESH)

    @pl.when(is_owner)
    def _():
        received(ym_in, ym_rs, YM, NPY)
        for d in range(IN_Z):
            for e in range(3 * E):
                ymat[d, e // E, e % E] = ym_in[pl.ds(d * YM + e, 8, stride=IN_Z * YM), :]
        mm, mz, mn = [[held(ymat, d, k) for d in range(IN_Z)] for k in range(3)]

        def keep(k, m):
            cmat[k] = m.reshape(E, 8, 128)

        phi = mm[0]()
        x = []
        for d in range(1, IN_Z):
            keep(3 + d, product(mz[d](), phi))
            phi = product(mm[d](), phi)
        keep(0, phi)
        x = held(cmat, 3 + IN_Z - 1)()
        for d in range(IN_Z - 2, 0, -1):
            x = held(cmat, 3 + d)() + product(mn[d](), x)
        keep(1, mz[0]() + product(mn[0](), x))
        n = mn[IN_Z - 1]()
        for d in range(IN_Z - 2, -1, -1):
            n = product(mn[d](), n)
        keep(2, n)

        received(yv_in, yv_rs, YV, NPY)
        v = [rows_of(yv_in, d * YV, IN_Z * YV) for d in range(IN_Z)]
        w = [rows_of(yv_in, d * YV + V, IN_Z * YV) for d in range(IN_Z)]
        e = v[0]
        ins = [None]
        for d in range(1, IN_Z):
            ins.append(e)
            e = v[d] + apply(mm[d](), e)
        g = w[IN_Z - 1] - apply(mz[IN_Z - 1](), ins[IN_Z - 1])
        for d in range(IN_Z - 2, -1, -1):
            g = w[d] + apply(mn[d](), g)
            if d:
                g = g - apply(mz[d](), ins[d])
        a, = chain([held(cmat, 0)], [e])
        g = g - apply(held(cmat, 1)(), a)
        b, = chain_back([held(cmat, 2)], [g])
        ins = [a]
        for d in range(IN_Z - 1):
            ins.append(v[d] + apply(mm[d](), ins[d]))
        ahead = [None] * IN_Z
        ahead[IN_Z - 1] = b
        for d in range(IN_Z - 1, 0, -1):
            ahead[d - 1] = w[d] - apply(mz[d](), ins[d]) + apply(mn[d](), ahead[d])
        for d in range(IN_Z):
            for c in range(V):
                yr_out[pl.ds(d * YV + c, 8, stride=IN_Z * YV), :] = ins[d][c]
                yr_out[pl.ds(d * YV + V + c, 8, stride=IN_Z * YV), :] = ahead[d][c]

        pltpu.make_async_copy(at(yr_out, py, YV), at(yr_in, z, YV), yr_rs.at[z]).start()

        def one(k, _):
            y_back(lax.rem(py + k, NPY)).start()
            return 0

        lax.fori_loop(1, NPY, one, 0)

    received(yr_in, yr_rs, YV, NPZ)

    def load_sy(j, _):
        return sy[j]

    def save_res(j, _, u):
        res[:, y_rows(j), :] = u

    forward_cells(load_sy, yl_v, y_rows, CY, (rows_of(yr_in, 0, YV),), save_fwy)
    backward_cells(load_fwy, yu_v, y_rows, CY, (rows_of(yr_in, V, YV),), save_res)
    written = pltpu.make_async_copy(res, out, out_s.at[0])
    written.start()

    x_sent(*xm)
    x_sent(*xv)
    x_sent(*xr)
    y_sent(*ym)
    y_sent(*yv)

    @pl.when(is_owner)
    def _():
        def one(k, _):
            y_back(lax.rem(py + k, NPY)).wait_send()
            return 0

        lax.fori_loop(1, NPY, one, 0)

    written.wait()


def per_device(field, forcing, *blocks):
    shape = field.shape
    args = [v.reshape(V, ROWS, 128) for v in (field, forcing)] + [m.reshape(E, ROWS, 128) for m in blocks]

    def vmem(*dims):
        return pltpu.VMEM(dims, F32)

    def dma(n):
        return pltpu.SemaphoreType.DMA((n,))

    scratch = [
        vmem(V, ROWS + 4 * CY, 128), vmem(V, ROWS, 128), *[vmem(E, ROWS, 128) for _ in range(6)], vmem(V, ROWS, 128),
        vmem(CY + 4, V, 8, 128), vmem(2, V, 2 * CY, 128), vmem(2, 2, V, 8, 128), vmem(V, ROWS, 128),
        vmem(CY, V, V, 8, 128), vmem(V, ROWS, 128), vmem(V, ROWS, 128), vmem(CY, V, 8, 128), vmem(CY, V, 8, 128),
        vmem(CY * XM, 128), vmem(NPX * XO * XM, 128),
        vmem(CY * XV, 128), vmem(NPX * XO * XV, 128), vmem(NPX * XO * XV, 128), vmem(CY * XV, 128),
        vmem(CX * YM, 128), vmem(NPY * YM, 128), vmem(CX * YV, 128), vmem(NPY * YV, 128), vmem(NPY * YV, 128), vmem(CX * YV, 128),
        vmem(XO, 3, E, 8, 128), vmem(IN_Z, 3, E, 8, 128), vmem(3 + IN_Z, E, 8, 128),
        dma(8), dma(4), dma(4), dma(NPX), dma(NPX), dma(NPX), dma(NPX), dma(NPX), dma(NPX),
        dma(NPZ), dma(NPY), dma(NPZ), dma(NPY), dma(NPY), dma(NPZ), dma(1),
    ]
    result = pl.pallas_call(
        kernel,
        out_shape=jax.ShapeDtypeStruct((V, ROWS, 128), F32),
        in_specs=[pl.BlockSpec(memory_space=pl.ANY)] * 8,
        out_specs=pl.BlockSpec(memory_space=pl.ANY),
        scratch_shapes=scratch,
        compiler_params=pltpu.CompilerParams(collective_id=0, has_side_effects=True),
        name="adi",
    )(*args)
    return result.reshape(shape)


def solution(mesh):
    vector, matrix = P(None, "px", "py", None), P(None, None, "px", "py", None)
    return jax.shard_map(
        per_device, mesh=mesh, in_specs=(vector,) * 2 + (matrix,) * 6, out_specs=vector, check_vma=False
    )
```

time: 786 us -> 48.5 us (0.06)
  the two profiles are of different devices: /device:TPU:124 before, /device:TPU:1 now
where the time goes in v1:
time: 48.5 us; the launch traced here: 48.4 us
  Pallas kernels  46.7 us (96%)
  local copies, waits for them, and re-layouts  1.72 us (4%)
    pallas_call x1, Pallas kernels, per_device(): pl.pallas_call(kernel, out_shape=jax.ShapeDtypeStruct((V, ROWS, 128), F32...  46.7 us
    unnamed x1, local copies, waits for them, and re-layouts  1.72 us

profile of v1, /device:TPU:1, one launch (start us, length us, event | category | flops | bytes accessed | tf_op | source)
XLA Modules:
  0.0 48.4 jit_solution(10442820857419378825)
XLA Ops:
  0.0 46.7 %adi.1 = f32[5,128,128]{2,1,0:T(8,128)} custom-call(f32[5,128,128]{2,1,0:T(8,128)} %bitcast.16, f32[5,128,128]{2,1,0:T(8,128)} %bitcast.17, f32[25,128,128]{2,1,0:T(8,128)} %bitcast.9, f32[25,128,128]{2,1,0:T(8,128)} %bitcast.10, f32[25,128,128]{2,1,0:T(8,128)} %bitcast.11, f32[25,128,128]{2,1,0:T(8,128)} %bitcast.12, f32[25,128,128]{2,1,0:T(8,128)} %bitcast.13, ...), custom_call_target="tpu_custom_call" | custom-call | tf_op jit(solution)/shard_map/adi/pallas_call | solution.py:481
  46.7 1.7 %copy.10 = f32[5,8,16,128]{3,2,1,0:T(8,128)} copy(f32[5,8,16,128]{3,2,1,0:T(8,128)} %bitcast.15) | data formatting | bytes 655360

commit v2 on v1

v2 whole, which is shorter than its diff:
```python
import jax
import jax.numpy as jnp
from jax import lax
from jax.experimental import pallas as pl
from jax.experimental.pallas import tpu as pltpu
from jax.sharding import PartitionSpec as P

DISSIPATION = 0.1
MESH = pl.DeviceIdType.MESH
F32 = jnp.float32

V = 5
E = V * V
NPX, NPY, NPZ = 8, 32, 8
IN_Z = NPY // NPZ
CX, CY = 8, 16
ROWS = CX * CY
XM, YM = 76, 80
XV, YV = 12, 16
YMP, YVP, YP = 88, 24, 24
XO = CY // NPX


def block(ref, rows):
    return ref[:, rows, :].reshape(V, V, 8, 128)


def total(terms):
    while len(terms) > 1:
        terms = [terms[k] + terms[k + 1] if k + 1 < len(terms) else terms[k] for k in range(0, len(terms), 2)]
    return terms[0]


def apply(m, x):
    return total([m[:, c] * x[c][None] for c in range(V)])


def product(m, b):
    rows = [total([m[a, c][None] * b[c] for c in range(V)]) for a in range(V)]
    return jnp.stack(rows)


def device_products(lo, up, up_again, n, psi, emit, before_up):
    first = lo(0)
    psi[0] = first

    def forward(i, m):
        m = product(lo(i), m)
        psi[i] = m
        return m

    last = lax.fori_loop(1, n, forward, first)
    emit(0, last)
    before_up()

    def backward(t, z):
        i = n - 2 - t
        return psi[i] + product(up(i), z)

    emit(E, lax.fori_loop(0, n - 1, backward, last))

    def upward(t, m):
        return product(up_again(n - 2 - t), m)

    emit(2 * E, lax.fori_loop(0, n - 1, upward, up(n - 1)))


def forward_cells(source, lo, n, start, save):
    def step(i, carry):
        out = []
        for t, f in enumerate(carry):
            cur = source(i, t)
            if f is not None:
                cur = cur - apply(lo(i, t), f)
            save(i, t, cur)
            out.append(cur)
        return tuple(out)

    begin = 0
    if start[0] is None:
        start, begin = step(0, start), 1
    return lax.fori_loop(begin, n, step, start)


def backward_cells(source, up, n, start, save):
    def step(k, carry):
        i = n - 1 - k
        out = []
        for t, g in enumerate(carry):
            cur = source(i, t)
            if g is not None:
                cur = cur - apply(up(i, t), g)
            if save is not None:
                save(i, t, cur)
            out.append(cur)
        return tuple(out)

    begin = 0
    if start[0] is None:
        start, begin = step(0, start), 1
    return lax.fori_loop(begin, n, step, start)


def kernel(field, forcing, xi, xl, xu, yi, yl, yu, out,
           fx, fo, xi_v, xl_v, xu_v, yi_v, yl_v, yu_v, yi_t, yl_t, yu_t,
           fy, hx, hy, rhs, psi, sx, fwx, sy, fwy,
           xm_out, xm_in, xv_out, xv_in, xr_out, xr_in,
           ym_out, ym_in, yv_out, yv_in, yr_out, yr_in, xmat, ymat, cmat,
           load_s, halo_ss, halo_rs, xm_ss, xm_rs, xv_ss, xv_rs, xr_ss, xr_rs,
           ym_ss, ym_rs, yv_ss, yv_rs, yr_ss, yr_rs):
    px, py = lax.axis_index("px"), lax.axis_index("py")
    core, z = lax.rem(px, 2), lax.div(py, IN_Z)

    def owner_of(r):
        return IN_Z * r + lax.rem(2 * core + r, IN_Z)

    is_owner = py == owner_of(z)

    mine = slice(2 * CY, 2 * CY + ROWS)

    def load(k, src, dst):
        return pltpu.make_async_copy(src, dst, load_s.at[k])

    padded = (slice(None), slice(None), slice(0, CY))
    in_xl, in_xu, in_field = load(0, xl, xl_v), load(1, xu, xu_v), load(2, field, fx.at[:, mine, :])
    in_yl, in_yu, in_yi = load(3, yl, yl_v.at[padded]), load(4, yu, yu_v.at[padded]), load(5, yi, yi_v.at[padded])
    in_fo, in_xi = load(6, forcing, fo), load(7, xi, xi_v)
    for c in (in_xl, in_xu, in_field):
        c.start()

    barrier = pltpu.get_barrier_semaphore()

    def greet_x(k, _):
        pl.semaphore_signal(barrier, inc=1, device_id=(lax.rem(px + k, NPX), py), device_id_type=MESH)
        return 0

    def greet_y(k, _):
        pl.semaphore_signal(barrier, inc=1, device_id=(px, lax.rem(py + k, NPY)), device_id_type=MESH)
        return 0

    lax.fori_loop(1, NPX, greet_x, 0)
    lax.fori_loop(1, NPY, greet_y, 0)

    def x_rows(i, h):
        return pl.ds(pl.multiple_of(CY * i + 8 * h, 8), 8)

    def y_rows(j):
        return pl.ds(j, 8, stride=CY)

    def turned(ref, j):
        return ref.reshape(E, CX * YP, 128)[:, pl.ds(j, 8, stride=YP), :].reshape(V, V, 8, 128)

    def x_block(ref):
        return lambda i, h: block(ref, x_rows(i, h))

    def y_block(ref):
        return lambda j, _=0: ref[j]

    def at(ref, k, size, pitch=None):
        return ref.at[pl.ds(pl.multiple_of(k * (pitch or size), 8), size), :]

    def x_copy(src, dst, ss, rs, size, k):
        return pltpu.make_async_remote_copy(
            at(src, k, size), at(dst, px, size), ss.at[k], rs.at[px], device_id=(k, py), device_id_type=MESH)

    def x_send_half(src, dst, ss, rs, size, half):
        first = 4 * half + lax.rem(px, 4)

        @pl.when(first == px)
        def _():
            pltpu.make_async_copy(at(src, px, size), at(dst, px, size), rs.at[px]).start()

        @pl.when(first != px)
        def _():
            x_copy(src, dst, ss, rs, size, first).start()

        for k in range(1, 4):
            x_copy(src, dst, ss, rs, size, 4 * half + lax.rem(px + k, 4)).start()

    def x_send(src, dst, ss, rs, size):
        pltpu.make_async_copy(at(src, px, size), at(dst, px, size), rs.at[px]).start()

        def one(k, _):
            x_copy(src, dst, ss, rs, size, lax.rem(px + k, NPX)).start()
            return 0

        lax.fori_loop(1, NPX, one, 0)

    def x_sent(src, dst, ss, rs, size):
        def one(k, _):
            x_copy(src, dst, ss, rs, size, lax.rem(px + k, NPX)).wait_send()
            return 0

        lax.fori_loop(1, NPX, one, 0)

    def received(dst, rs, size, count, pitch=None):
        def one(k, _):
            pltpu.make_async_copy(at(dst, k, size, pitch), at(dst, k, size, pitch), rs.at[k]).wait()
            return 0

        lax.fori_loop(0, count, one, 0)

    def slot(d):
        return NPZ * lax.rem(d, IN_Z) + lax.div(d, IN_Z)

    def y_copy(src, dst, ss, rs, size, pitch, r):
        return pltpu.make_async_remote_copy(
            at(src, r, size, pitch), at(dst, slot(py), size, pitch), ss.at[r], rs.at[slot(py)],
            device_id=(px, owner_of(r)), device_id_type=MESH)

    def y_send(src, dst, ss, rs, size, pitch):
        @pl.when(is_owner)
        def _():
            pltpu.make_async_copy(at(src, z, size, pitch), at(dst, slot(py), size, pitch), rs.at[slot(py)]).start()

        @pl.when(jnp.logical_not(is_owner))
        def _():
            y_copy(src, dst, ss, rs, size, pitch, z).start()

        def one(k, _):
            y_copy(src, dst, ss, rs, size, pitch, lax.rem(z + k, NPZ)).start()
            return 0

        lax.fori_loop(1, NPZ, one, 0)

    def y_sent(src, dst, ss, rs, size, pitch):
        @pl.when(jnp.logical_not(is_owner))
        def _():
            y_copy(src, dst, ss, rs, size, pitch, z).wait_send()

        def one(k, _):
            y_copy(src, dst, ss, rs, size, pitch, lax.rem(z + k, NPZ)).wait_send()
            return 0

        lax.fori_loop(1, NPZ, one, 0)

    xm = (xm_out, xm_in, xm_ss, xm_rs, XO * XM)
    xv = (xv_out, xv_in, xv_ss, xv_rs, XO * XV)
    xr = (xr_out, xr_in, xr_ss, xr_rs, XO * XV)
    ym = (ym_out, ym_in, ym_ss, ym_rs, YM, YMP)
    yv = (yv_out, yv_in, yv_ss, yv_rs, YV, YVP)
    in_field.wait()

    def turn(j, _):
        fy[2 + j] = fx[:, pl.ds(2 * CY + j, 8, stride=CY), :]
        return 0

    lax.fori_loop(0, CY, turn, 0)

    right, left = lax.rem(px + 1, NPX), lax.rem(px + NPX - 1, NPX)
    north, south = lax.rem(py + 1, NPY), lax.rem(py + NPY - 1, NPY)
    halos = [
        pltpu.make_async_remote_copy(a, b, halo_ss.at[k], halo_rs.at[k], device_id=d, device_id_type=MESH)
        for k, (a, b, d) in enumerate([
            (fx.at[:, ROWS : ROWS + 2 * CY, :], hx.at[0], (right, py)),
            (fx.at[:, 2 * CY : 4 * CY, :], hx.at[1], (left, py)),
            (fy.at[CY : CY + 2], hy.at[0], (px, north)),
            (fy.at[2:4], hy.at[1], (px, south))])
    ]
    in_xl.wait()
    in_yl.start()
    in_yu.start()
    for h in range(2):
        def emit(base, m, h=h):
            for e in range(E):
                xm_out[pl.ds(8 * h * XM + base + e, 8, stride=XM), :] = m[e // V, e % V]

        def before_up(h=h):
            if h == 0:
                in_xu.wait()
                for c in (in_fo, in_xi, in_yi):
                    c.start()

        lo, up = [lambda i, ref=ref, h=h: block(ref, x_rows(i, h)) for ref in (xl_v, xu_v)]
        device_products(lo, up, up, CX, psi, emit, before_up)
        if h == 0:
            pl.semaphore_wait(barrier, NPX + NPY - 2)
            for c in halos:
                c.start()
        x_send_half(*xm, h)

    in_yl.wait()

    def emit_y(base, m):
        for e in range(E):
            ym_out[pl.ds(base + e, 8, stride=YMP), :] = m[e // V, e % V]

    def lo_y(j):
        m = turned(yl_v, j)
        yl_t[j] = m
        return m

    def up_y(j):
        m = turned(yu_v, j)
        yu_t[j] = m
        return m

    device_products(lo_y, up_y, y_block(yu_t), CY, psi, emit_y, in_yu.wait)
    y_send(*ym)

    in_fo.wait()
    for c in halos:
        c.wait()
    fx[:, 0 : 2 * CY, :] = jnp.where(px == 0, 0.0, hx[0])
    fx[:, 2 * CY + ROWS :, :] = jnp.where(px == NPX - 1, 0.0, hx[1])
    fy[0:2] = jnp.where(py == 0, 0.0, hy[0])
    fy[CY + 2 :] = jnp.where(py == NPY - 1, 0.0, hy[1])

    def difference(v):
        return v[0] - 4.0 * v[1] + 6.0 * v[2] - 4.0 * v[3] + v[4]

    def along_y(j, _):
        d = difference([fy[j + k] for k in range(5)])
        rhs[:, y_rows(j), :] = fo[:, y_rows(j), :] - DISSIPATION * d
        return 0

    lax.fori_loop(0, CY, along_y, 0)
    in_xi.wait()

    def x_source(i, h):
        d = difference([fx[:, x_rows(i + k, h), :] for k in range(5)])
        s = apply(block(xi_v, x_rows(i, h)), rhs[:, x_rows(i, h), :] - DISSIPATION * d)
        sx[:, x_rows(i, h), :] = s
        return s

    def save_fwx(i, h, f):
        fwx[:, x_rows(i, h), :] = f

    def load_fwx(i, h):
        return fwx[:, x_rows(i, h), :]

    ends = forward_cells(x_source, x_block(xl_v), CX, (None, None), save_fwx)
    starts = backward_cells(load_fwx, x_block(xu_v), CX, (None, None), None)
    for h in range(2):
        for c in range(V):
            xv_out[pl.ds(8 * h * XV + c, 8, stride=XV), :] = ends[h][c]
            xv_out[pl.ds(8 * h * XV + V + c, 8, stride=XV), :] = starts[h][c]
    x_send(*xv)

    place = lax.broadcasted_iota(jnp.int32, (V, 8, 128), 1)

    def chain(m, v):
        def one(_, a):
            return tuple(jnp.where(place == 0, 0.0, pltpu.roll(vk + apply(mk(), ak), 1, axis=1))
                         for vk, mk, ak in zip(v, m, a))

        return lax.fori_loop(0, 7, one, tuple(jnp.zeros((V, 8, 128), F32) for _ in v))

    def chain_back(m, v):
        def one(_, b):
            return tuple(jnp.where(place == 7, 0.0, pltpu.roll(vk + apply(mk(), bk), 7, axis=1))
                         for vk, mk, bk in zip(v, m, b))

        return lax.fori_loop(0, 7, one, tuple(jnp.zeros((V, 8, 128), F32) for _ in v))

    def held(ref, *at_):
        return lambda: ref[at_].reshape(V, V, 8, 128)

    in_yi.wait()

    def turn_yi(j, _):
        yi_t[j] = turned(yi_v, j)
        return 0

    lax.fori_loop(0, CY, turn_yi, 0)

    received(xm_in, xm_rs, XO * XM, NPX)
    for r in range(XO):
        for e in range(3 * E):
            xmat[r, e // E, e % E] = xm_in[pl.ds(r * XM + e, 8, stride=XO * XM), :]
    received(xv_in, xv_rs, XO * XV, NPX)

    def rows_of(ref, first, stride):
        return jnp.stack([ref[pl.ds(first + c, 8, stride=stride), :] for c in range(V)])

    v = [rows_of(xv_in, r * XV, XO * XV) for r in range(XO)]
    w = [rows_of(xv_in, r * XV + V, XO * XV) for r in range(XO)]
    a = chain([held(xmat, r, 0) for r in range(XO)], v)
    w = [w[r] - apply(held(xmat, r, 1)(), a[r]) for r in range(XO)]
    b = chain_back([held(xmat, r, 2) for r in range(XO)], w)
    for r in range(XO):
        for c in range(V):
            xr_out[pl.ds(r * XV + c, 8, stride=XO * XV), :] = a[r][c]
            xr_out[pl.ds(r * XV + V + c, 8, stride=XO * XV), :] = b[r][c]
    x_send(*xr)
    received(xr_in, xr_rs, XO * XV, NPX)

    before = tuple(rows_of(xr_in, 8 * h * XV, XV) for h in range(2))
    after = tuple(rows_of(xr_in, 8 * h * XV + V, XV) for h in range(2))

    def load_sx(i, h):
        return sx[:, x_rows(i, h), :]

    forward_cells(load_sx, x_block(xl_v), CX, before, save_fwx)
    backward_cells(load_fwx, x_block(xu_v), CX, after, save_fwx)

    def y_source(j, _):
        s = apply(yi_t[j], fwx[:, y_rows(j), :])
        sy[j] = s
        return s

    def save_fwy(j, _, f):
        fwy[j] = f

    def load_fwy(j, _):
        return fwy[j]

    end, = forward_cells(y_source, y_block(yl_t), CY, (None,), save_fwy)
    start, = backward_cells(load_fwy, y_block(yu_t), CY, (None,), None)
    for c in range(V):
        yv_out[pl.ds(c, 8, stride=YVP), :] = end[c]
        yv_out[pl.ds(V + c, 8, stride=YVP), :] = start[c]
    y_send(*yv)

    def y_back(d):
        return pltpu.make_async_remote_copy(
            at(yr_out, slot(d), YV, YVP), at(yr_in, z, YV, YVP), yr_ss.at[d], yr_rs.at[z], device_id=(px, d), device_id_type=MESH)

    @pl.when(is_owner)
    def _():
        received(ym_in, ym_rs, YM, NPY, YMP)
        for d in range(IN_Z):
            for e in range(3 * E):
                ymat[d, e // E, e % E] = ym_in[pl.ds(d * NPZ * YMP + e, 8, stride=YMP), :]
        mm, mz, mn = [[held(ymat, d, k) for d in range(IN_Z)] for k in range(3)]

        def keep(k, m):
            cmat[k] = m.reshape(E, 8, 128)

        phi = mm[0]()
        x = []
        for d in range(1, IN_Z):
            keep(3 + d, product(mz[d](), phi))
            phi = product(mm[d](), phi)
        keep(0, phi)
        x = held(cmat, 3 + IN_Z - 1)()
        for d in range(IN_Z - 2, 0, -1):
            x = held(cmat, 3 + d)() + product(mn[d](), x)
        keep(1, mz[0]() + product(mn[0](), x))
        n = mn[IN_Z - 1]()
        for d in range(IN_Z - 2, -1, -1):
            n = product(mn[d](), n)
        keep(2, n)

        received(yv_in, yv_rs, YV, NPY, YVP)
        v = [rows_of(yv_in, d * NPZ * YVP, YVP) for d in range(IN_Z)]
        w = [rows_of(yv_in, d * NPZ * YVP + V, YVP) for d in range(IN_Z)]
        e = v[0]
        ins = [None]
        for d in range(1, IN_Z):
            ins.append(e)
            e = v[d] + apply(mm[d](), e)
        g = w[IN_Z - 1] - apply(mz[IN_Z - 1](), ins[IN_Z - 1])
        for d in range(IN_Z - 2, -1, -1):
            g = w[d] + apply(mn[d](), g)
            if d:
                g = g - apply(mz[d](), ins[d])
        a, = chain([held(cmat, 0)], [e])
        g = g - apply(held(cmat, 1)(), a)
        b, = chain_back([held(cmat, 2)], [g])
        ins = [a]
        for d in range(IN_Z - 1):
            ins.append(v[d] + apply(mm[d](), ins[d]))
        ahead = [None] * IN_Z
        ahead[IN_Z - 1] = b
        for d in range(IN_Z - 1, 0, -1):
            ahead[d - 1] = w[d] - apply(mz[d](), ins[d]) + apply(mn[d](), ahead[d])
        for d in range(IN_Z):
            for c in range(V):
                yr_out[pl.ds(d * NPZ * YVP + c, 8, stride=YVP), :] = ins[d][c]
                yr_out[pl.ds(d * NPZ * YVP + V + c, 8, stride=YVP), :] = ahead[d][c]

        pltpu.make_async_copy(at(yr_out, slot(py), YV, YVP), at(yr_in, z, YV, YVP), yr_rs.at[z]).start()

        def one(k, _):
            y_back(lax.rem(py + k, NPY)).start()
            return 0

        lax.fori_loop(1, NPY, one, 0)

    received(yr_in, yr_rs, YV, NPZ, YVP)

    def load_sy(j, _):
        return sy[j]

    def save_res(j, _, u):
        out[:, y_rows(j), :] = u

    forward_cells(load_sy, y_block(yl_t), CY, (rows_of(yr_in, 0, YVP),), save_fwy)
    backward_cells(load_fwy, y_block(yu_t), CY, (rows_of(yr_in, V, YVP),), save_res)

    x_sent(*xm)
    x_sent(*xv)
    x_sent(*xr)
    y_sent(*ym)
    y_sent(*yv)

    @pl.when(is_owner)
    def _():
        def one(k, _):
            y_back(lax.rem(py + k, NPY)).wait_send()
            return 0

        lax.fori_loop(1, NPY, one, 0)


def per_device(field, forcing, *blocks):
    shape = field.shape
    args = [v.reshape(V, ROWS, 128) for v in (field, forcing)] + [m.reshape(E, ROWS, 128) for m in blocks[:3]]
    args += [m.reshape(E, CX, CY, 128) for m in blocks[3:]]

    def vmem(*dims):
        return pltpu.VMEM(dims, F32)

    def dma(n):
        return pltpu.SemaphoreType.DMA((n,))

    scratch = [
        vmem(V, ROWS + 4 * CY, 128), vmem(V, ROWS, 128), *[vmem(E, ROWS, 128) for _ in range(3)],
        *[vmem(E, CX, YP, 128) for _ in range(3)], *[vmem(CY, V, V, 8, 128) for _ in range(3)],
        vmem(CY + 4, V, 8, 128), vmem(2, V, 2 * CY, 128), vmem(2, 2, V, 8, 128), vmem(V, ROWS, 128),
        vmem(CY, V, V, 8, 128), vmem(V, ROWS, 128), vmem(V, ROWS, 128), vmem(CY, V, 8, 128), vmem(CY, V, 8, 128),
        vmem(CY * XM, 128), vmem(NPX * XO * XM, 128),
        vmem(CY * XV, 128), vmem(NPX * XO * XV, 128), vmem(NPX * XO * XV, 128), vmem(CY * XV, 128),
        vmem(CX * YMP, 128), vmem(NPY * YMP, 128),
        vmem(CX * YVP, 128), vmem(NPY * YVP, 128), vmem(NPY * YVP, 128), vmem(CX * YVP, 128),
        vmem(XO, 3, E, 8, 128), vmem(IN_Z, 3, E, 8, 128), vmem(3 + IN_Z, E, 8, 128),
        dma(8), dma(4), dma(4), dma(NPX), dma(NPX), dma(NPX), dma(NPX), dma(NPX), dma(NPX),
        dma(NPZ), dma(NPY), dma(NPZ), dma(NPY), dma(NPY), dma(NPZ),
    ]
    result = pl.pallas_call(
        kernel,
        out_shape=jax.ShapeDtypeStruct((V, ROWS, 128), F32),
        in_specs=[pl.BlockSpec(memory_space=pltpu.HBM)] * 8,
        out_specs=pl.BlockSpec(memory_space=pltpu.VMEM),
        scratch_shapes=scratch,
        compiler_params=pltpu.CompilerParams(collective_id=0, has_side_effects=True),
        name="adi",
    )(*args)
    return result.reshape(shape)


def solution(mesh):
    vector, matrix = P(None, "px", "py", None), P(None, None, "px", "py", None)
    return jax.shard_map(
        per_device, mesh=mesh, in_specs=(vector,) * 2 + (matrix,) * 6, out_specs=vector, check_vma=False
    )
```

time: 48.5 us -> 45.4 us (0.936)
  Pallas kernels: 46.7 us -> 43.5 us
    pallas_call x1, Pallas kernels: 46.7 us -> 43.5 us  [per_device(): pl.pallas_call(kernel, out_shape=jax.ShapeDtypeStruct((V, ROWS, 128), F32...]
where the time goes in v2:
time: 45.4 us; the launch traced here: 45.3 us
  Pallas kernels  43.5 us (96%)
  local copies, waits for them, and re-layouts  1.72 us (4%)
    pallas_call x1, Pallas kernels, per_device(): pl.pallas_call(kernel, out_shape=jax.ShapeDtypeStruct((V, ROWS, 128), F32...  43.5 us
    unnamed x1, local copies, waits for them, and re-layouts  1.72 us

profile of v2, /device:TPU:1, one launch (start us, length us, event | category | flops | bytes accessed | tf_op | source)
XLA Modules:
  0.0 45.3 jit_solution(1424836756935915982)
XLA Ops:
  0.0 43.5 %adi.1 = f32[5,128,128]{2,1,0:T(8,128)} custom-call(f32[5,128,128]{2,1,0:T(8,128)} %bitcast.16, f32[5,128,128]{2,1,0:T(8,128)} %bitcast.17, f32[25,128,128]{2,1,0:T(8,128)} %bitcast.9, f32[25,128,128]{2,1,0:T(8,128)} %bitcast.10, f32[25,128,128]{2,1,0:T(8,128)} %bitcast.11, f32[25,8,16,128]{3,2,1,0:T(8,128)} %bitcast.12, f32[25,8,16,128]{3,2,1,0:T(8,128)} %bitcast.13, ...), custom_call_target="tpu_custom_call" | custom-call | tf_op jit(solution)/shard_map/adi/pallas_call | solution.py:531
  43.5 1.7 %copy.10 = f32[5,8,16,128]{3,2,1,0:T(8,128)} copy(f32[5,8,16,128]{3,2,1,0:T(8,128)} %bitcast.15) | data formatting | bytes 655360

commit v3 on v2

--- a/solution.py
+++ b/solution.py
@@ -18,6 +18,7 @@
 XM, YM = 76, 80
 XV, YV = 12, 16
 YMP, YVP, YP = 88, 24, 24
+CHIPS = NPX // 2
 XO = CY // NPX
 
 
@@ -40,7 +41,7 @@
     return jnp.stack(rows)
 
 
-def device_products(lo, up, up_again, n, psi, emit, before_up):
+def device_products(lo, up, up_again, n, psi, emit, before_up=lambda: None):
     first = lo(0)
     psi[0] = first
 
@@ -104,12 +105,13 @@
 def kernel(field, forcing, xi, xl, xu, yi, yl, yu, out,
            fx, fo, xi_v, xl_v, xu_v, yi_v, yl_v, yu_v, yi_t, yl_t, yu_t,
            fy, hx, hy, rhs, psi, sx, fwx, sy, fwy,
-           xm_out, xm_in, xv_out, xv_in, xr_out, xr_in,
+           pm, pv, xm_out, xm_in, xv_out, xv_in, xr_out, xr_in,
            ym_out, ym_in, yv_out, yv_in, yr_out, yr_in, xmat, ymat, cmat,
-           load_s, halo_ss, halo_rs, xm_ss, xm_rs, xv_ss, xv_rs, xr_ss, xr_rs,
+           load_s, halo_ss, halo_rs, pair_ss, pair_rs, xm_ss, xm_rs, xv_ss, xv_rs, xr_ss, xr_rs,
            ym_ss, ym_rs, yv_ss, yv_rs, yr_ss, yr_rs):
     px, py = lax.axis_index("px"), lax.axis_index("py")
-    core, z = lax.rem(px, 2), lax.div(py, IN_Z)
+    core, chip, z = lax.rem(px, 2), lax.div(px, 2), lax.div(py, IN_Z)
+    partner = px + 1 - 2 * core
 
     def owner_of(r):
         return IN_Z * r + lax.rem(2 * core + r, IN_Z)
@@ -159,39 +161,34 @@
     def at(ref, k, size, pitch=None):
         return ref.at[pl.ds(pl.multiple_of(k * (pitch or size), 8), size), :]
 
-    def x_copy(src, dst, ss, rs, size, k):
+    def x_copy(src, dst, ss, rs, size, c):
         return pltpu.make_async_remote_copy(
-            at(src, k, size), at(dst, px, size), ss.at[k], rs.at[px], device_id=(k, py), device_id_type=MESH)
-
-    def x_send_half(src, dst, ss, rs, size, half):
-        first = 4 * half + lax.rem(px, 4)
-
-        @pl.when(first == px)
-        def _():
-            pltpu.make_async_copy(at(src, px, size), at(dst, px, size), rs.at[px]).start()
-
-        @pl.when(first != px)
-        def _():
-            x_copy(src, dst, ss, rs, size, first).start()
-
-        for k in range(1, 4):
-            x_copy(src, dst, ss, rs, size, 4 * half + lax.rem(px + k, 4)).start()
+            at(src, c, size), at(dst, chip, size), ss.at[c], rs.at[chip],
+            device_id=(2 * c + core, py), device_id_type=MESH)
+
+    def other_chip(k):
+        return lax.rem(chip + k, CHIPS)
 
     def x_send(src, dst, ss, rs, size):
-        pltpu.make_async_copy(at(src, px, size), at(dst, px, size), rs.at[px]).start()
-
-        def one(k, _):
-            x_copy(src, dst, ss, rs, size, lax.rem(px + k, NPX)).start()
-            return 0
-
-        lax.fori_loop(1, NPX, one, 0)
+        for k in range(1, CHIPS):
+            x_copy(src, dst, ss, rs, size, other_chip(k)).start()
+        pltpu.make_async_copy(at(src, chip, size), at(dst, chip, size), rs.at[chip]).start()
 
     def x_sent(src, dst, ss, rs, size):
-        def one(k, _):
-            x_copy(src, dst, ss, rs, size, lax.rem(px + k, NPX)).wait_send()
-            return 0
-
-        lax.fori_loop(1, NPX, one, 0)
+        for k in range(1, CHIPS):
+            x_copy(src, dst, ss, rs, size, other_chip(k)).wait_send()
+
+    def x_back(k):
+        d = lax.rem(px + k, NPX)
+        return pltpu.make_async_remote_copy(
+            at(xr_out, lax.div(d, 2), XO * XV), at(xr_in, CHIPS * core + chip, XO * XV), xr_ss.at[d],
+            xr_rs.at[CHIPS * core + chip], device_id=(d, py), device_id_type=MESH)
+
+    def pair_copy(k, ref):
+        return pltpu.make_async_remote_copy(
+            ref, ref, pair_ss.at[k], pair_rs.at[k], device_id=(partner, py), device_id_type=MESH)
+
+    pairs = [pair_copy(0, pm.at[core, 1 - core]), pair_copy(1, pm.at[core, core]), pair_copy(2, pv.at[core])]
 
     def received(dst, rs, size, count, pitch=None):
         def one(k, _):
@@ -236,7 +233,6 @@
 
     xm = (xm_out, xm_in, xm_ss, xm_rs, XO * XM)
     xv = (xv_out, xv_in, xv_ss, xv_rs, XO * XV)
-    xr = (xr_out, xr_in, xr_ss, xr_rs, XO * XV)
     ym = (ym_out, ym_in, ym_ss, ym_rs, YM, YMP)
     yv = (yv_out, yv_in, yv_ss, yv_rs, YV, YVP)
     in_field.wait()
@@ -260,43 +256,40 @@
     in_xl.wait()
     in_yl.start()
     in_yu.start()
-    for h in range(2):
+    for first, h in ((True, 1 - core), (False, core)):
         def emit(base, m, h=h):
-            for e in range(E):
-                xm_out[pl.ds(8 * h * XM + base + e, 8, stride=XM), :] = m[e // V, e % V]
-
-        def before_up(h=h):
-            if h == 0:
+            pm[core, h, pl.ds(base, E)] = m.reshape(E, 8, 128)
+
+        def before_up(first=first):
+            if first:
                 in_xu.wait()
                 for c in (in_fo, in_xi, in_yi):
                     c.start()
 
         lo, up = [lambda i, ref=ref, h=h: block(ref, x_rows(i, h)) for ref in (xl_v, xu_v)]
         device_products(lo, up, up, CX, psi, emit, before_up)
-        if h == 0:
+        if first:
             pl.semaphore_wait(barrier, NPX + NPY - 2)
+            pairs[0].start()
             for c in halos:
                 c.start()
-        x_send_half(*xm, h)
-
-    in_yl.wait()
-
-    def emit_y(base, m):
+        else:
+            pairs[1].start()
+
+    pairs[0].wait()
+
+    def half(d, k):
+        return pm[d, core, pl.ds(k * E, E)].reshape(V, V, 8, 128)
+
+    def emit_x(base, m):
         for e in range(E):
-            ym_out[pl.ds(base + e, 8, stride=YMP), :] = m[e // V, e % V]
-
-    def lo_y(j):
-        m = turned(yl_v, j)
-        yl_t[j] = m
-        return m
-
-    def up_y(j):
-        m = turned(yu_v, j)
-        yu_t[j] = m
-        return m
-
-    device_products(lo_y, up_y, y_block(yu_t), CY, psi, emit_y, in_yu.wait)
-    y_send(*ym)
+            xm_out[pl.ds(base + e, 8, stride=XM), :] = m[e // V, e % V]
+
+    m0, n0 = half(0, 0), half(0, 2)
+    emit_x(0, product(half(1, 0), m0))
+    emit_x(E, half(0, 1) + product(n0, product(half(1, 1), m0)))
+    emit_x(2 * E, product(n0, half(1, 2)))
+    x_send(*xm)
 
     in_fo.wait()
     for c in halos:
@@ -332,26 +325,57 @@
     ends = forward_cells(x_source, x_block(xl_v), CX, (None, None), save_fwx)
     starts = backward_cells(load_fwx, x_block(xu_v), CX, (None, None), None)
     for h in range(2):
-        for c in range(V):
-            xv_out[pl.ds(8 * h * XV + c, 8, stride=XV), :] = ends[h][c]
-            xv_out[pl.ds(8 * h * XV + V + c, 8, stride=XV), :] = starts[h][c]
+        pv[core, h, pl.ds(0, V)] = ends[h]
+        pv[core, h, pl.ds(V, V)] = starts[h]
+    pairs[2].start()
+
+    in_yl.wait()
+
+    def emit_y(base, m):
+        for e in range(E):
+            ym_out[pl.ds(base + e, 8, stride=YMP), :] = m[e // V, e % V]
+
+    def lo_y(j):
+        m = turned(yl_v, j)
+        yl_t[j] = m
+        return m
+
+    def up_y(j):
+        m = turned(yu_v, j)
+        yu_t[j] = m
+        return m
+
+    device_products(lo_y, up_y, y_block(yu_t), CY, psi, emit_y, in_yu.wait)
+    y_send(*ym)
+
+    pairs[2].wait()
+
+    def part(d, h, k):
+        return pv[d, h, pl.ds(k * V, V)]
+
+    v0 = part(0, core, 0)
+    v = part(1, core, 0) + apply(half(1, 0), v0)
+    w = part(0, core, 1) + apply(half(0, 2), part(1, core, 1) - apply(half(1, 1), v0))
+    for c in range(V):
+        xv_out[pl.ds(c, 8, stride=XV), :] = v[c]
+        xv_out[pl.ds(V + c, 8, stride=XV), :] = w[c]
     x_send(*xv)
 
     place = lax.broadcasted_iota(jnp.int32, (V, 8, 128), 1)
 
-    def chain(m, v):
+    def chain(m, v, by, count):
         def one(_, a):
-            return tuple(jnp.where(place == 0, 0.0, pltpu.roll(vk + apply(mk(), ak), 1, axis=1))
+            return tuple(jnp.where(place < by, 0.0, pltpu.roll(vk + apply(mk(), ak), by, axis=1))
                          for vk, mk, ak in zip(v, m, a))
 
-        return lax.fori_loop(0, 7, one, tuple(jnp.zeros((V, 8, 128), F32) for _ in v))
-
-    def chain_back(m, v):
+        return lax.fori_loop(0, count, one, tuple(jnp.zeros((V, 8, 128), F32) for _ in v))
+
+    def chain_back(m, v, by, count):
         def one(_, b):
-            return tuple(jnp.where(place == 7, 0.0, pltpu.roll(vk + apply(mk(), bk), 7, axis=1))
+            return tuple(jnp.where(place >= 8 - by, 0.0, pltpu.roll(vk + apply(mk(), bk), 8 - by, axis=1))
                          for vk, mk, bk in zip(v, m, b))
 
-        return lax.fori_loop(0, 7, one, tuple(jnp.zeros((V, 8, 128), F32) for _ in v))
+        return lax.fori_loop(0, count, one, tuple(jnp.zeros((V, 8, 128), F32) for _ in v))
 
     def held(ref, *at_):
         return lambda: ref[at_].reshape(V, V, 8, 128)
@@ -364,35 +388,43 @@
 
     lax.fori_loop(0, CY, turn_yi, 0)
 
-    received(xm_in, xm_rs, XO * XM, NPX)
-    for r in range(XO):
-        for e in range(3 * E):
-            xmat[r, e // E, e % E] = xm_in[pl.ds(r * XM + e, 8, stride=XO * XM), :]
-    received(xv_in, xv_rs, XO * XV, NPX)
+    received(xm_in, xm_rs, XO * XM, CHIPS)
+    for e in range(3 * E):
+        xmat[e // E, e % E] = xm_in[pl.ds(e, 8, stride=XM), :]
+    received(xv_in, xv_rs, XO * XV, CHIPS)
 
     def rows_of(ref, first, stride):
         return jnp.stack([ref[pl.ds(first + c, 8, stride=stride), :] for c in range(V)])
 
-    v = [rows_of(xv_in, r * XV, XO * XV) for r in range(XO)]
-    w = [rows_of(xv_in, r * XV + V, XO * XV) for r in range(XO)]
-    a = chain([held(xmat, r, 0) for r in range(XO)], v)
-    w = [w[r] - apply(held(xmat, r, 1)(), a[r]) for r in range(XO)]
-    b = chain_back([held(xmat, r, 2) for r in range(XO)], w)
-    for r in range(XO):
-        for c in range(V):
-            xr_out[pl.ds(r * XV + c, 8, stride=XO * XV), :] = a[r][c]
-            xr_out[pl.ds(r * XV + V + c, 8, stride=XO * XV), :] = b[r][c]
-    x_send(*xr)
+    a, = chain([held(xmat, 0)], [rows_of(xv_in, 0, XV)], XO, CHIPS - 1)
+    b, = chain_back([held(xmat, 2)], [rows_of(xv_in, V, XV) - apply(held(xmat, 1)(), a)], XO, CHIPS - 1)
+    for c in range(V):
+        xr_out[pl.ds(c, 8, stride=XV), :] = a[c]
+        xr_out[pl.ds(V + c, 8, stride=XV), :] = b[c]
+    own = CHIPS * core + chip
+    pltpu.make_async_copy(at(xr_out, chip, XO * XV), at(xr_in, own, XO * XV), xr_rs.at[own]).start()
+    for k in range(1, NPX):
+        x_back(k).start()
+    pairs[1].wait()
     received(xr_in, xr_rs, XO * XV, NPX)
 
-    before = tuple(rows_of(xr_in, 8 * h * XV, XV) for h in range(2))
-    after = tuple(rows_of(xr_in, 8 * h * XV + V, XV) for h in range(2))
+    before, after = [], []
+    for h in range(2):
+        a, b = rows_of(xr_in, 8 * h * XV, XV), rows_of(xr_in, 8 * h * XV + V, XV)
+
+        def of(d, k, h=h):
+            return pm[d, h, pl.ds(k * E, E)].reshape(V, V, 8, 128)
+
+        a1 = part(0, h, 0) + apply(of(0, 0), a)
+        b0 = part(1, h, 1) - apply(of(1, 1), a1) + apply(of(1, 2), b)
+        before.append(jnp.where(core == 0, a, a1))
+        after.append(jnp.where(core == 0, b0, b))
 
     def load_sx(i, h):
         return sx[:, x_rows(i, h), :]
 
-    forward_cells(load_sx, x_block(xl_v), CX, before, save_fwx)
-    backward_cells(load_fwx, x_block(xu_v), CX, after, save_fwx)
+    forward_cells(load_sx, x_block(xl_v), CX, tuple(before), save_fwx)
+    backward_cells(load_fwx, x_block(xu_v), CX, tuple(after), save_fwx)
 
     def y_source(j, _):
         s = apply(yi_t[j], fwx[:, y_rows(j), :])
@@ -455,9 +487,9 @@
             g = w[d] + apply(mn[d](), g)
             if d:
                 g = g - apply(mz[d](), ins[d])
-        a, = chain([held(cmat, 0)], [e])
+        a, = chain([held(cmat, 0)], [e], 1, NPZ - 1)
         g = g - apply(held(cmat, 1)(), a)
-        b, = chain_back([held(cmat, 2)], [g])
+        b, = chain_back([held(cmat, 2)], [g], 1, NPZ - 1)
         ins = [a]
         for d in range(IN_Z - 1):
             ins.append(v[d] + apply(mm[d](), ins[d]))
@@ -491,7 +523,8 @@
 
     x_sent(*xm)
     x_sent(*xv)
-    x_sent(*xr)
+    for k in range(1, NPX):
+        x_back(k).wait_send()
     y_sent(*ym)
     y_sent(*yv)
 
@@ -520,12 +553,12 @@
         *[vmem(E, CX, YP, 128) for _ in range(3)], *[vmem(CY, V, V, 8, 128) for _ in range(3)],
         vmem(CY + 4, V, 8, 128), vmem(2, V, 2 * CY, 128), vmem(2, 2, V, 8, 128), vmem(V, ROWS, 128),
         vmem(CY, V, V, 8, 128), vmem(V, ROWS, 128), vmem(V, ROWS, 128), vmem(CY, V, 8, 128), vmem(CY, V, 8, 128),
-        vmem(CY * XM, 128), vmem(NPX * XO * XM, 128),
-        vmem(CY * XV, 128), vmem(NPX * XO * XV, 128), vmem(NPX * XO * XV, 128), vmem(CY * XV, 128),
+        vmem(2, 2, 3 * E, 8, 128), vmem(2, 2, 2 * V, 8, 128), vmem(8 * XM, 128), vmem(8 * XM, 128),
+        vmem(8 * XV, 128), vmem(8 * XV, 128), vmem(8 * XV, 128), vmem(CY * XV, 128),
         vmem(CX * YMP, 128), vmem(NPY * YMP, 128),
         vmem(CX * YVP, 128), vmem(NPY * YVP, 128), vmem(NPY * YVP, 128), vmem(CX * YVP, 128),
-        vmem(XO, 3, E, 8, 128), vmem(IN_Z, 3, E, 8, 128), vmem(3 + IN_Z, E, 8, 128),
-        dma(8), dma(4), dma(4), dma(NPX), dma(NPX), dma(NPX), dma(NPX), dma(NPX), dma(NPX),
+        vmem(3, E, 8, 128), vmem(IN_Z, 3, E, 8, 128), vmem(3 + IN_Z, E, 8, 128),
+        dma(8), dma(4), dma(4), dma(3), dma(3), dma(CHIPS), dma(CHIPS), dma(CHIPS), dma(CHIPS), dma(NPX), dma(NPX),
         dma(NPZ), dma(NPY), dma(NPZ), dma(NPY), dma(NPY), dma(NPZ),
     ]
     result = pl.pallas_call(
@@ -534,7 +567,7 @@
         in_specs=[pl.BlockSpec(memory_space=pltpu.HBM)] * 8,
         out_specs=pl.BlockSpec(memory_space=pltpu.VMEM),
         scratch_shapes=scratch,
-        compiler_params=pltpu.CompilerParams(collective_id=0, has_side_effects=True),
+        compiler_params=pltpu.CompilerParams(collective_id=0, has_side_effects=True, vmem_limit_bytes=56000000),
         name="adi",
     )(*args)
     return result.reshape(shape)

time: 45.4 us -> 42.6 us (0.938)
  Pallas kernels: 43.5 us -> 41.4 us
  local copies, waits for them, and re-layouts: 1.72 us -> 0.73 us
    pallas_call x1, Pallas kernels: 43.5 us -> 41.4 us  [per_device(): pl.pallas_call(kernel, out_shape=jax.ShapeDtypeStruct((V, ROWS, 128), F32...]
    unnamed x1, local copies, waits for them, and re-layouts: 1.72 us -> 0.73 us
where the time goes in v3:
time: 42.6 us; the launch traced here: 42.1 us
  Pallas kernels  41.4 us (97%)
  local copies, waits for them, and re-layouts  0.73 us (2%)
    pallas_call x1, Pallas kernels, per_device(): pl.pallas_call(kernel, out_shape=jax.ShapeDtypeStruct((V, ROWS, 128), F32...  41.4 us

profile of v3, /device:TPU:1, one launch (start us, length us, event | category | flops | bytes accessed | tf_op | source)
XLA Modules:
  0.0 42.1 jit_solution(5121310156574676217)
XLA Ops:
  0.0 41.4 %adi.1 = f32[5,128,128]{2,1,0:T(8,128)S(1)} custom-call(f32[5,128,128]{2,1,0:T(8,128)} %bitcast.16, f32[5,128,128]{2,1,0:T(8,128)} %bitcast.17, f32[25,128,128]{2,1,0:T(8,128)} %bitcast.10, f32[25,128,128]{2,1,0:T(8,128)} %bitcast.11, f32[25,128,128]{2,1,0:T(8,128)} %bitcast.12, f32[25,8,16,128]{3,2,1,0:T(8,128)} %bitcast.13, f32[25,8,16,128]{3,2,1,0:T(8,128)} %bitcast.14, ...), custom_call_target="tpu_custom_call" | custom-call | tf_op jit(solution)/shard_map/adi/pallas_call | solution.py:564
  41.4 0.7 %copy.10 = f32[5,8,16,128]{3,2,1,0:T(8,128)} copy(f32[5,8,16,128]{3,2,1,0:T(8,128)S(1)} %bitcast.9) | data formatting | bytes 655360

commit v4 on v3

--- a/solution.py
+++ b/solution.py
@@ -15,8 +15,8 @@
 IN_Z = NPY // NPZ
 CX, CY = 8, 16
 ROWS = CX * CY
-XM, YM = 76, 80
-XV, YV = 12, 16
+XM, YM = 76, 75
+XV, YV = 12, 10
 YMP, YVP, YP = 88, 24, 24
 CHIPS = NPX // 2
 XO = CY // NPX
@@ -170,7 +170,7 @@
         return lax.rem(chip + k, CHIPS)
 
     def x_send(src, dst, ss, rs, size):
-        for k in range(1, CHIPS):
+        for k in (2, 1, 3):
             x_copy(src, dst, ss, rs, size, other_chip(k)).start()
         pltpu.make_async_copy(at(src, chip, size), at(dst, chip, size), rs.at[chip]).start()
 
@@ -179,7 +179,7 @@
             x_copy(src, dst, ss, rs, size, other_chip(k)).wait_send()
 
     def x_back(k):
-        d = lax.rem(px + k, NPX)
+        d = 2 * other_chip(k // 2) + lax.rem(core + k, 2)
         return pltpu.make_async_remote_copy(
             at(xr_out, lax.div(d, 2), XO * XV), at(xr_in, CHIPS * core + chip, XO * XV), xr_ss.at[d],
             xr_rs.at[CHIPS * core + chip], device_id=(d, py), device_id_type=MESH)
@@ -206,6 +206,9 @@
             device_id=(px, owner_of(r)), device_id_type=MESH)
 
     def y_send(src, dst, ss, rs, size, pitch):
+        for k in (4, 3, 5, 2, 6, 1, 7):
+            y_copy(src, dst, ss, rs, size, pitch, lax.rem(z + k, NPZ)).start()
+
         @pl.when(is_owner)
         def _():
             pltpu.make_async_copy(at(src, z, size, pitch), at(dst, slot(py), size, pitch), rs.at[slot(py)]).start()
@@ -213,12 +216,6 @@
         @pl.when(jnp.logical_not(is_owner))
         def _():
             y_copy(src, dst, ss, rs, size, pitch, z).start()
-
-        def one(k, _):
-            y_copy(src, dst, ss, rs, size, pitch, lax.rem(z + k, NPZ)).start()
-            return 0
-
-        lax.fori_loop(1, NPZ, one, 0)
 
     def y_sent(src, dst, ss, rs, size, pitch):
         @pl.when(jnp.logical_not(is_owner))
@@ -276,6 +273,25 @@
         else:
             pairs[1].start()
 
+    in_yl.wait()
+
+    def emit_y(base, m):
+        for e in range(E):
+            ym_out[pl.ds(base + e, 8, stride=YMP), :] = m[e // V, e % V]
+
+    def lo_y(j):
+        m = turned(yl_v, j)
+        yl_t[j] = m
+        return m
+
+    def up_y(j):
+        m = turned(yu_v, j)
+        yu_t[j] = m
+        return m
+
+    device_products(lo_y, up_y, y_block(yu_t), CY, psi, emit_y, in_yu.wait)
+    y_send(*ym)
+
     pairs[0].wait()
 
     def half(d, k):
@@ -329,25 +345,6 @@
         pv[core, h, pl.ds(V, V)] = starts[h]
     pairs[2].start()
 
-    in_yl.wait()
-
-    def emit_y(base, m):
-        for e in range(E):
-            ym_out[pl.ds(base + e, 8, stride=YMP), :] = m[e // V, e % V]
-
-    def lo_y(j):
-        m = turned(yl_v, j)
-        yl_t[j] = m
-        return m
-
-    def up_y(j):
-        m = turned(yu_v, j)
-        yu_t[j] = m
-        return m
-
-    device_products(lo_y, up_y, y_block(yu_t), CY, psi, emit_y, in_yu.wait)
-    y_send(*ym)
-
     pairs[2].wait()
 
     def part(d, h, k):
@@ -403,7 +400,7 @@
         xr_out[pl.ds(V + c, 8, stride=XV), :] = b[c]
     own = CHIPS * core + chip
     pltpu.make_async_copy(at(xr_out, chip, XO * XV), at(xr_in, own, XO * XV), xr_rs.at[own]).start()
-    for k in range(1, NPX):
+    for k in (4, 5, 2, 3, 6, 7, 1):
         x_back(k).start()
     pairs[1].wait()
     received(xr_in, xr_rs, XO * XV, NPX)
@@ -502,13 +499,11 @@
                 yr_out[pl.ds(d * NPZ * YVP + c, 8, stride=YVP), :] = ins[d][c]
                 yr_out[pl.ds(d * NPZ * YVP + V + c, 8, stride=YVP), :] = ahead[d][c]
 
+        for dz in (4, 3, 5, 2, 6, 1, 7, 0):
+            for dy in (2, 1, 3, 0):
+                if dz or dy:
+                    y_back(IN_Z * lax.rem(z + dz, NPZ) + lax.rem(py + dy, IN_Z)).start()
         pltpu.make_async_copy(at(yr_out, slot(py), YV, YVP), at(yr_in, z, YV, YVP), yr_rs.at[z]).start()
-
-        def one(k, _):
-            y_back(lax.rem(py + k, NPY)).start()
-            return 0
-
-        lax.fori_loop(1, NPY, one, 0)
 
     received(yr_in, yr_rs, YV, NPZ, YVP)
 

time: 42.6 us -> 39.1 us (0.918)
  Pallas kernels: 41.4 us -> 38.2 us
    pallas_call x1, Pallas kernels: 41.4 us -> 38.2 us  [per_device(): pl.pallas_call(kernel, out_shape=jax.ShapeDtypeStruct((V, ROWS, 128), F32...]
where the time goes in v4:
time: 39.1 us; the launch traced here: 39 us
  Pallas kernels  38.2 us (98%)
  local copies, waits for them, and re-layouts  0.73 us (2%)
    pallas_call x1, Pallas kernels, per_device(): pl.pallas_call(kernel, out_shape=jax.ShapeDtypeStruct((V, ROWS, 128), F32...  38.2 us

profile of v4, /device:TPU:1, one launch (start us, length us, event | category | flops | bytes accessed | tf_op | source)
XLA Modules:
  0.0 39.0 jit_solution(16503618012501619619)
XLA Ops:
  0.0 38.2 %adi.1 = f32[5,128,128]{2,1,0:T(8,128)S(1)} custom-call(f32[5,128,128]{2,1,0:T(8,128)} %bitcast.16, f32[5,128,128]{2,1,0:T(8,128)} %bitcast.17, f32[25,128,128]{2,1,0:T(8,128)} %bitcast.10, f32[25,128,128]{2,1,0:T(8,128)} %bitcast.11, f32[25,128,128]{2,1,0:T(8,128)} %bitcast.12, f32[25,8,16,128]{3,2,1,0:T(8,128)} %bitcast.13, f32[25,8,16,128]{3,2,1,0:T(8,128)} %bitcast.14, ...), custom_call_target="tpu_custom_call" | custom-call | tf_op jit(solution)/shard_map/adi/pallas_call | solution.py:559
  38.2 0.7 %copy.10 = f32[5,8,16,128]{3,2,1,0:T(8,128)} copy(f32[5,8,16,128]{3,2,1,0:T(8,128)S(1)} %bitcast.9) | data formatting | bytes 655360

commit v5 on v4

--- a/solution.py
+++ b/solution.py
@@ -132,16 +132,13 @@
 
     barrier = pltpu.get_barrier_semaphore()
 
-    def greet_x(k, _):
+    for dz in (4, 3, 5, 2, 6, 1, 7, 0):
+        for dy in (2, 1, 3, 0):
+            if dz or dy:
+                other = IN_Z * lax.rem(z + dz, NPZ) + lax.rem(py + dy, IN_Z)
+                pl.semaphore_signal(barrier, inc=1, device_id=(px, other), device_id_type=MESH)
+    for k in (4, 5, 3, 2, 6, 1, 7):
         pl.semaphore_signal(barrier, inc=1, device_id=(lax.rem(px + k, NPX), py), device_id_type=MESH)
-        return 0
-
-    def greet_y(k, _):
-        pl.semaphore_signal(barrier, inc=1, device_id=(px, lax.rem(py + k, NPY)), device_id_type=MESH)
-        return 0
-
-    lax.fori_loop(1, NPX, greet_x, 0)
-    lax.fori_loop(1, NPY, greet_y, 0)
 
     def x_rows(i, h):
         return pl.ds(pl.multiple_of(CY * i + 8 * h, 8), 8)
@@ -505,17 +502,6 @@
                     y_back(IN_Z * lax.rem(z + dz, NPZ) + lax.rem(py + dy, IN_Z)).start()
         pltpu.make_async_copy(at(yr_out, slot(py), YV, YVP), at(yr_in, z, YV, YVP), yr_rs.at[z]).start()
 
-    received(yr_in, yr_rs, YV, NPZ, YVP)
-
-    def load_sy(j, _):
-        return sy[j]
-
-    def save_res(j, _, u):
-        out[:, y_rows(j), :] = u
-
-    forward_cells(load_sy, y_block(yl_t), CY, (rows_of(yr_in, 0, YVP),), save_fwy)
-    backward_cells(load_fwy, y_block(yu_t), CY, (rows_of(yr_in, V, YVP),), save_res)
-
     x_sent(*xm)
     x_sent(*xv)
     for k in range(1, NPX):
@@ -530,6 +516,17 @@
             return 0
 
         lax.fori_loop(1, NPY, one, 0)
+
+    received(yr_in, yr_rs, YV, NPZ, YVP)
+
+    def load_sy(j, _):
+        return sy[j]
+
+    def save_res(j, _, u):
+        out[:, y_rows(j), :] = u
+
+    forward_cells(load_sy, y_block(yl_t), CY, (rows_of(yr_in, 0, YVP),), save_fwy)
+    backward_cells(load_fwy, y_block(yu_t), CY, (rows_of(yr_in, V, YVP),), save_res)
 
 
 def per_device(field, forcing, *blocks):

time: 39.1 us -> 38.6 us (0.987)
  Pallas kernels: 38.2 us -> 37.8 us
    pallas_call x1, Pallas kernels: 38.2 us -> 37.8 us  [per_device(): pl.pallas_call(kernel, out_shape=jax.ShapeDtypeStruct((V, ROWS, 128), F32...]
where the time goes in v5:
time: 38.6 us; the launch traced here: 38.5 us
  Pallas kernels  37.8 us (98%)
  local copies, waits for them, and re-layouts  0.73 us (2%)
    pallas_call x1, Pallas kernels, per_device(): pl.pallas_call(kernel, out_shape=jax.ShapeDtypeStruct((V, ROWS, 128), F32...  37.8 us

profile of v5, /device:TPU:1, one launch (start us, length us, event | category | flops | bytes accessed | tf_op | source)
XLA Modules:
  0.0 38.5 jit_solution(7059194412395566478)
XLA Ops:
  0.0 37.8 %adi.1 = f32[5,128,128]{2,1,0:T(8,128)S(1)} custom-call(f32[5,128,128]{2,1,0:T(8,128)} %bitcast.16, f32[5,128,128]{2,1,0:T(8,128)} %bitcast.17, f32[25,128,128]{2,1,0:T(8,128)} %bitcast.10, f32[25,128,128]{2,1,0:T(8,128)} %bitcast.11, f32[25,128,128]{2,1,0:T(8,128)} %bitcast.12, f32[25,8,16,128]{3,2,1,0:T(8,128)} %bitcast.13, f32[25,8,16,128]{3,2,1,0:T(8,128)} %bitcast.14, ...), custom_call_target="tpu_custom_call" | custom-call | tf_op jit(solution)/shard_map/adi/pallas_call | solution.py:556
  37.8 0.7 %copy.10 = f32[5,8,16,128]{3,2,1,0:T(8,128)} copy(f32[5,8,16,128]{3,2,1,0:T(8,128)S(1)} %bitcast.9) | data formatting | bytes 655360

commit v6 on v5

--- a/solution.py
+++ b/solution.py
@@ -10,6 +10,7 @@
 F32 = jnp.float32
 
 V = 5
+UNROLL = 4
 E = V * V
 NPX, NPY, NPZ = 8, 32, 8
 IN_Z = NPY // NPZ
@@ -80,7 +81,7 @@
     begin = 0
     if start[0] is None:
         start, begin = step(0, start), 1
-    return lax.fori_loop(begin, n, step, start)
+    return lax.fori_loop(begin, n, step, start, unroll=UNROLL)
 
 
 def backward_cells(source, up, n, start, save):
@@ -99,7 +100,7 @@
     begin = 0
     if start[0] is None:
         start, begin = step(0, start), 1
-    return lax.fori_loop(begin, n, step, start)
+    return lax.fori_loop(begin, n, step, start, unroll=UNROLL)
 
 
 def kernel(field, forcing, xi, xl, xu, yi, yl, yu, out,

time: 38.6 us -> 38.2 us (0.990)
  Pallas kernels: 37.8 us -> 37.4 us
where the time goes in v6:
time: 38.2 us
  Pallas kernels  37.4 us (98%)
  local copies, waits for them, and re-layouts  0.73 us (2%)
    pallas_call x1, Pallas kernels, per_device(): pl.pallas_call(kernel, out_shape=jax.ShapeDtypeStruct((V, ROWS, 128), F32...  37.4 us

profile of v6, /device:TPU:1, one launch (start us, length us, event | category | flops | bytes accessed | tf_op | source)
XLA Modules:
  0.0 38.2 jit_solution(6446798699913145763)
XLA Ops:
  0.0 37.4 %adi.1 = f32[5,128,128]{2,1,0:T(8,128)S(1)} custom-call(f32[5,128,128]{2,1,0:T(8,128)} %bitcast.16, f32[5,128,128]{2,1,0:T(8,128)} %bitcast.17, f32[25,128,128]{2,1,0:T(8,128)} %bitcast.10, f32[25,128,128]{2,1,0:T(8,128)} %bitcast.11, f32[25,128,128]{2,1,0:T(8,128)} %bitcast.12, f32[25,8,16,128]{3,2,1,0:T(8,128)} %bitcast.13, f32[25,8,16,128]{3,2,1,0:T(8,128)} %bitcast.14, ...), custom_call_target="tpu_custom_call" | custom-call | tf_op jit(solution)/shard_map/adi/pallas_call | solution.py:557
  37.4 0.7 %copy.10 = f32[5,8,16,128]{3,2,1,0:T(8,128)} copy(f32[5,8,16,128]{3,2,1,0:T(8,128)S(1)} %bitcast.9) | data formatting | bytes 655360

commit v7 on v6

--- a/solution.py
+++ b/solution.py
@@ -363,14 +363,14 @@
             return tuple(jnp.where(place < by, 0.0, pltpu.roll(vk + apply(mk(), ak), by, axis=1))
                          for vk, mk, ak in zip(v, m, a))
 
-        return lax.fori_loop(0, count, one, tuple(jnp.zeros((V, 8, 128), F32) for _ in v))
+        return lax.fori_loop(0, count, one, tuple(jnp.zeros((V, 8, 128), F32) for _ in v), unroll=True)
 
     def chain_back(m, v, by, count):
         def one(_, b):
             return tuple(jnp.where(place >= 8 - by, 0.0, pltpu.roll(vk + apply(mk(), bk), 8 - by, axis=1))
                          for vk, mk, bk in zip(v, m, b))
 
-        return lax.fori_loop(0, count, one, tuple(jnp.zeros((V, 8, 128), F32) for _ in v))
+        return lax.fori_loop(0, count, one, tuple(jnp.zeros((V, 8, 128), F32) for _ in v), unroll=True)
 
     def held(ref, *at_):
         return lambda: ref[at_].reshape(V, V, 8, 128)

time: 38.2 us -> 38.2 us (level)
  no operation moved by 1% of the time
where the time goes in v7:
time: 38.2 us; the launch traced here: 38.1 us
  Pallas kernels  37.3 us (98%)
  local copies, waits for them, and re-layouts  0.73 us (2%)
    pallas_call x1, Pallas kernels, per_device(): pl.pallas_call(kernel, out_shape=jax.ShapeDtypeStruct((V, ROWS, 128), F32...  37.3 us

profile of v7, /device:TPU:1, one launch (start us, length us, event | category | flops | bytes accessed | tf_op | source)
XLA Modules:
  0.0 38.1 jit_solution(2327043283491451125)
XLA Ops:
  0.0 37.3 %adi.1 = f32[5,128,128]{2,1,0:T(8,128)S(1)} custom-call(f32[5,128,128]{2,1,0:T(8,128)} %bitcast.16, f32[5,128,128]{2,1,0:T(8,128)} %bitcast.17, f32[25,128,128]{2,1,0:T(8,128)} %bitcast.10, f32[25,128,128]{2,1,0:T(8,128)} %bitcast.11, f32[25,128,128]{2,1,0:T(8,128)} %bitcast.12, f32[25,8,16,128]{3,2,1,0:T(8,128)} %bitcast.13, f32[25,8,16,128]{3,2,1,0:T(8,128)} %bitcast.14, ...), custom_call_target="tpu_custom_call" | custom-call | tf_op jit(solution)/shard_map/adi/pallas_call | solution.py:557
  37.4 0.7 %copy.10 = f32[5,8,16,128]{3,2,1,0:T(8,128)} copy(f32[5,8,16,128]{3,2,1,0:T(8,128)S(1)} %bitcast.9) | data formatting | bytes 655360
